TPU v7x, 32 devices: a whole 2x2x4 slice. The times are simulated.
32 devices in a mesh: groups: 2 (over x), tok: 16 (over z, y, core).
Axes of the slice: x: 2, y: 2, z: 4, core: 2. Of those that a mesh axis runs over, the one named last changes fastest.
Arguments:
- vis_query: bfloat16 [8192, 1280], P(('groups', 'tok')), parts along dimension 0, may hold values from -180 to 180
- vis_keyvalue: bfloat16 [2, 8192, 1280], P(None, ('groups', 'tok')), parts along dimension 1, may hold values from -6 to 6
- vis_residual: bfloat16 [8192, 1280], P(('groups', 'tok')), parts along dimension 0, may hold values from -4 to 4
- vis_out_weight: bfloat16 [1280, 1280], P('tok'), may hold values from -0.15625 to 0.15625
- vis_out_bias: float32 [1280], replicated, may hold values from -4 to 4
- image_units: int32 [96], P('groups'), parts along dimension 0, may hold values from 1 to 32, 1024 in all
- text_embed: bfloat16 [8192, 5120], P(('groups', 'tok')), parts along dimension 0, may hold values from -6 to 6
- lm_gain: float32 [5120], replicated, may hold values from 0.1 to 1.9
- lm_kv_weight: bfloat16 [5120, 2048], P(None, 'tok'), may hold values from -0.078125 to 0.078125
- lm_kv_bias: float32 [2048], replicated, may hold values from -6 to 6
- text_positions: int32 [8192], P(('groups', 'tok')), parts along dimension 0, may hold values from 0 to 4095
- image_destination: int32 [2048, 1], P(('groups', 'tok')), parts along dimension 0, may hold values from 0 to 15; in each aligned block of 64 rows (0 to 63, 64 to 127, ...) at most 8 rows name the same one
- image_positions: int32 [3, 4096], P(None, ('groups', 'tok')), parts along dimension 1, may hold values from 0 to 4095
Outputs:
- text_cache: bfloat16 [8192, 2048], P(('groups', 'tok')), parts along dimension 0
- image_cache: bfloat16 [4096, 2048], P(('groups', 'tok')), parts along dimension 0
There are 2 independent parts, one for each index of `groups`. A program takes and returns all parts, laid end to end along the dimension named above; an argument that names none is the same for every part. Nothing has to cross between parts.
Inputs may be any that keep to these rules, and one draw needn't show every extreme that they name: `image_units`: each image spans whole merged rows; entries sum to 1024 and one reaches the largest value. `image_destination`: among the 64 rows of one device no destination appears more than 8 times, and some device's rows reach that count.
All inputs are finite; a program needn't handle non-finite values.
Results may differ from a plain program's by a relative error of at most 0.0052.
Values may be sent and summed in bfloat16 or wider, within the bound.
No kernel may reach another device: no remote copies, remote signals or barrier semaphores. Data moves between devices by JAX's collectives and lax.ppermute only.
A program may use at most 128 MiB of HBM per device.

v0:
```python
import functools
import math

import jax
import jax.numpy as jnp
from jax import lax
from jax.experimental import pallas as pl
from jax.experimental.pallas import tpu as pltpu
from jax.sharding import PartitionSpec as P


VIS_HEADS = 16
KV_HEADS = 8
LM_HEAD = 128


norm_epsilon = 1e-06
rope_base = 1000000.0


def with_halo(block, sides, width):
    for axis, dim in sides:
        count = lax.axis_size(axis)
        forward = [(i, i + 1) for i in range(count - 1)]
        backward = [(target, source) for source, target in forward]
        low = lax.ppermute(
            lax.slice_in_dim(block, block.shape[dim] - width, None, axis=dim), axis, forward
        )
        high = lax.ppermute(lax.slice_in_dim(block, 0, width, axis=dim), axis, backward)
        block = jnp.concatenate([low, block, high], axis=dim)
    return block


def segment_ids(global_index, bounds):
    return jnp.sum((global_index[:, None] >= bounds[None, :]).astype(jnp.int32), axis=1) - 1


def rms_scale(rows, gain):
    values = rows.astype(jnp.float32)
    mean_square = jnp.mean(values * values, axis=1, keepdims=True)
    return (values * lax.rsqrt(mean_square + norm_epsilon) * gain).astype(jnp.bfloat16)


def rotation_tables(positions):
    half_size = LM_HEAD // 2
    index_pair = jnp.arange(half_size, dtype=jnp.int32)
    frequency = jnp.power(jnp.float32(rope_base), -2.0 * index_pair.astype(jnp.float32) / LM_HEAD)
    section = (index_pair >= half_size // 4).astype(jnp.int32) + (
        index_pair >= half_size // 4 + 3 * half_size // 8
    ).astype(jnp.int32)
    places = positions.astype(jnp.float32)
    chosen = jnp.zeros((positions.shape[1], half_size), jnp.float32)
    for axis_number in range(3):
        chosen = (
            chosen
            + places[axis_number][:, None] * (section == axis_number).astype(jnp.float32)[None, :]
        )
    angles = chosen * frequency[None, :]
    return jnp.cos(angles), jnp.sin(angles)


def rotate_keys(values, bias, positions):
    shifted = values + bias
    row_count = shifted.shape[0]
    kv_half = shifted.shape[1] // 2
    half_size = LM_HEAD // 2
    key_part = shifted[:, :kv_half].reshape(row_count, KV_HEADS, LM_HEAD)
    lower_half = key_part[:, :, :half_size]
    upper_half = key_part[:, :, half_size:]
    cosine, sine_part = rotation_tables(positions)
    cosine, sine_part = cosine[:, None, :], sine_part[:, None, :]
    turned = jnp.concatenate(
        [
            lower_half * cosine - upper_half * sine_part,
            upper_half * cosine + lower_half * sine_part,
        ],
        axis=2,
    )
    return jnp.concatenate(
        [turned.reshape(row_count, kv_half), shifted[:, kv_half:]], axis=1
    ).astype(jnp.bfloat16)


def head_attention(query_head, key_head, value_head, allowed, score_scale):
    scores = (
        jnp.einsum("qd,kd->qk", query_head, key_head, preferred_element_type=jnp.float32)
        * score_scale
    )
    scores = jnp.where(allowed, scores, -1e30)
    row_max = jnp.max(scores, axis=1, keepdims=True)
    shifted = jnp.exp(scores - row_max)
    weights = (shifted / jnp.sum(shifted, axis=1, keepdims=True)).astype(jnp.bfloat16)
    return jnp.dot(weights, value_head, preferred_element_type=jnp.float32).astype(jnp.bfloat16)


def project_rows(normed, kv_weight):
    return jnp.dot(
        normed,
        lax.all_gather(kv_weight, "tok", axis=1, tiled=True),
        preferred_element_type=jnp.float32,
    )


def ranks_of(target):
    unit_count = target.shape[0]
    same_target = target[:, None] == target[None, :]
    earlier = (
        jnp.arange(unit_count, dtype=jnp.int32)[None, :]
        < jnp.arange(unit_count, dtype=jnp.int32)[:, None]
    )
    return jnp.sum((same_target & earlier).astype(jnp.int32), axis=1)


def per_device_gathered(
    vis_query,
    vis_keyvalue,
    vis_residual,
    vis_out_weight,
    vis_out_bias,
    image_units,
    text_embed,
    lm_gain,
    lm_kv_weight,
    lm_kv_bias,
    text_positions,
    image_destination,
    image_positions,
):
    patch_count, vis_width = vis_query.shape
    head_size = vis_width // VIS_HEADS
    half_window = patch_count // 2
    device_count = lax.axis_size("tok")
    device_index = lax.axis_index("tok")
    nearby = with_halo(vis_keyvalue, (("tok", 1),), half_window)
    bounds = jnp.concatenate([jnp.zeros((1,), jnp.int32), jnp.cumsum(4 * image_units)])
    offset = device_index * patch_count
    query_ids = segment_ids(offset + jnp.arange(patch_count, dtype=jnp.int32), bounds)
    key_ids = segment_ids(
        offset - half_window + jnp.arange(2 * patch_count, dtype=jnp.int32), bounds
    )
    allowed = query_ids[:, None] == key_ids[None, :]
    score_scale = 1.0 / math.sqrt(head_size)
    query_heads = vis_query.reshape(patch_count, VIS_HEADS, head_size).transpose(1, 0, 2)
    key_heads = nearby[0].reshape(2 * patch_count, VIS_HEADS, head_size).transpose(1, 0, 2)
    value_heads = nearby[1].reshape(2 * patch_count, VIS_HEADS, head_size).transpose(1, 0, 2)
    attended = lax.map(
        lambda pieces: head_attention(pieces[0], pieces[1], pieces[2], allowed, score_scale),
        (query_heads, key_heads, value_heads),
    )
    attended = attended.transpose(1, 0, 2).reshape(patch_count, vis_width)
    projected = jnp.dot(
        attended,
        lax.all_gather(vis_out_weight, "tok", axis=0, tiled=True),
        preferred_element_type=jnp.float32,
    )
    vis_hidden = (projected + vis_out_bias + vis_residual.astype(jnp.float32)).astype(jnp.bfloat16)
    merged = vis_hidden.reshape(patch_count // 4, 4 * vis_width)
    target = image_destination[:, 0]
    slot_count = image_positions.shape[1]
    capacity = slot_count // device_count
    slot_index = target * capacity + ranks_of(target)
    text_count = text_embed.shape[0]
    kv_width = lm_kv_bias.shape[0]
    normed = rms_scale(jnp.concatenate([text_embed, merged], axis=0), lm_gain)
    projected_rows = project_rows(normed, lm_kv_weight)
    text_values = projected_rows[:text_count]
    outgoing = (
        jnp.zeros((slot_count, kv_width), jnp.float32)
        .at[slot_index]
        .set(projected_rows[text_count:])
    )
    image_values = lax.all_to_all(outgoing, "tok", split_axis=0, concat_axis=0, tiled=True)
    text_cache = rotate_keys(
        text_values, lm_kv_bias, jnp.broadcast_to(text_positions[None, :], (3, text_count))
    )
    image_cache = rotate_keys(image_values, lm_kv_bias, image_positions)
    return (text_cache, image_cache)


def call_kernel(body, outs, *args, specs=None, scratch=(), cost=None, limit=10):
    flops, moved = cost if cost else (0, 0)
    return pl.pallas_call(
        body,
        out_shape=outs,
        grid=(1,) if specs else (),
        in_specs=specs or [pl.BlockSpec(memory_space=pltpu.VMEM)] * len(args),
        out_specs=jax.tree.map(lambda _: pl.BlockSpec(memory_space=pltpu.VMEM), outs),
        scratch_shapes=list(scratch),
        cost_estimate=pl.CostEstimate(flops=flops, bytes_accessed=moved, transcendentals=0),
        compiler_params=pltpu.CompilerParams(vmem_limit_bytes=limit << 20),
    )(*args)


def attention_body(query, own, low, high, units, attended, *, head_size, window):
    patch_count, width = query.shape
    half = patch_count // 2
    count = units.shape[1]
    first = lax.axis_index("tok") * patch_count
    wide = lax.broadcasted_iota(jnp.int32, (count, count), 0)
    across = lax.broadcasted_iota(jnp.int32, (count, count), 1)
    units_col = jnp.sum(jnp.where(wide == across, units[...], 0), axis=1, keepdims=True)
    ends_row = 4 * jnp.sum(jnp.where(wide <= across, units_col, 0), axis=0, keepdims=True)
    ends_col = 4 * jnp.sum(jnp.where(across <= wide, units[...], 0), axis=1, keepdims=True)
    patch = first + lax.broadcasted_iota(jnp.int32, (patch_count, 1), 0)
    query_ids = jnp.sum((patch >= ends_row).astype(jnp.int32), axis=1, keepdims=True)
    near = first - half + lax.broadcasted_iota(jnp.int32, (1, 2 * patch_count), 1)
    key_ids = jnp.sum((near >= ends_col).astype(jnp.int32), axis=0, keepdims=True)
    key_ids = jnp.where(near < 0, -1, key_ids)
    score_scale = 1.0 / math.sqrt(head_size)
    allowed = [
        query_ids[b * half : (b + 1) * half] == key_ids[:, b * half : (b + 3) * half]
        for b in range(2)
    ]
    sides = (low, high)
    contract = (((1,), (1,)), ((), ()))

    def one_head(head, carry):
        begin = pl.multiple_of(
            jnp.minimum((head * head_size) // LM_HEAD * LM_HEAD, width - window), LM_HEAD
        )
        columns = pl.ds(begin, window)
        lane = lax.broadcasted_iota(jnp.int32, (1, window), 1) + begin
        mine = (lane >= head * head_size) & (lane < (head + 1) * head_size)
        picked = jnp.where(mine, query[:, columns], 0)
        middle = lax.dot_general(
            picked, own[0, :, columns], contract, preferred_element_type=jnp.float32
        )
        for b in range(2):
            rows = slice(b * half, (b + 1) * half)
            edge = lax.dot_general(
                picked[rows], sides[b][0, :, columns], contract, preferred_element_type=jnp.float32
            )
            parts = [edge, middle[rows]] if b == 0 else [middle[rows], edge]
            scores = jnp.concatenate(parts, axis=1) * score_scale
            scores = jnp.where(allowed[b], scores, -1e30)
            shifted = jnp.exp(scores - jnp.max(scores, axis=1, keepdims=True))
            weights = (shifted / jnp.sum(shifted, axis=1, keepdims=True)).astype(jnp.bfloat16)
            split = half if b == 0 else 2 * half
            pieces = (low[1, :, columns], own[1, :, columns])
            if b == 1:
                pieces = (own[1, :, columns], high[1, :, columns])
            mixed = jnp.dot(
                weights[:, :split], pieces[0], preferred_element_type=jnp.float32
            ) + jnp.dot(weights[:, split:], pieces[1], preferred_element_type=jnp.float32)
            attended[rows, columns] = jnp.where(
                mine, mixed.astype(jnp.bfloat16), attended[rows, columns]
            )
        return carry

    lax.fori_loop(0, width // head_size, one_head, 0)


def normed_rows(values, gain):
    mean_square = jnp.mean(values * values, axis=1, keepdims=True)
    return (values * lax.rsqrt(mean_square + norm_epsilon) * gain).astype(jnp.bfloat16)


def norm_body(rows, gain, normed):
    normed[...] = normed_rows(rows[...].astype(jnp.float32), gain[...])


def places():
    me = lax.axis_index("tok")
    return me % 2, me // 2 % 2, me // 4


def hidden_body(first, second, *refs):
    pieces, (bias, residual, gain, normed, weight, hidden) = refs[:-6], refs[-6:]
    core, line, floor = places()
    rings = len(pieces) // 2
    for number, piece in enumerate(pieces):
        pair, depth, _ = piece.shape
        parity = core if number < rings else 1 - core
        level = lax.rem(floor - number % rings + rings, rings)
        for part in range(pair):
            head = level * 4 + (line ^ part) * 2 + parity
            weight[pl.ds(pl.multiple_of(head * depth, 16), depth), :] = piece[part]
    split = first.shape[1]
    total = jnp.dot(first[...], weight[:split], preferred_element_type=jnp.float32)
    total = total + jnp.dot(second[...], weight[split:], preferred_element_type=jnp.float32)
    total = total + bias[...] + residual[...].astype(jnp.float32)
    total = total.astype(jnp.bfloat16).astype(jnp.float32)
    tiles, units = hidden.shape[0], hidden.shape[1] // 4
    for tile in range(tiles):
        hidden[tile] = total[:, tile * LM_HEAD : (tile + 1) * LM_HEAD]
    merged = jnp.concatenate(
        [
            hidden[tile, pl.ds(part, units, stride=4), :]
            for part in range(4)
            for tile in range(tiles)
        ],
        axis=1,
    )
    normed[...] = normed_rows(merged, gain[...])


def pair_product(side, rows, pieces):
    if len(pieces) == 2:
        weight = jnp.concatenate([pieces[0][...], pieces[1][...]], axis=1)
        return jnp.dot(rows[...], weight, preferred_element_type=jnp.float32)
    depth = pieces[0].shape[0]
    total = None
    for number in range(2):
        begin = side if number == 0 else 1 - side
        columns = pl.ds(pl.multiple_of(begin * depth, LM_HEAD), depth)
        weight = jnp.concatenate(
            [pieces[2 * number][...], pieces[2 * number + 1][...]], axis=1
        )
        term = jnp.dot(rows[:, columns], weight, preferred_element_type=jnp.float32)
        total = term if total is None else total + term
    return total


def project_body(*refs, sizes, first):
    inputs = 4 + sum(sizes)
    sources, (bias, cosine, sine, place) = refs[:inputs], refs[inputs : inputs + 4]
    out_own, out_other, out_image = refs[inputs + 4 : inputs + 7]
    rows, held, arrived = refs[inputs + 7], refs[inputs + 8 : -1], refs[-1]
    targets, begin = [], 0
    for source in sources[:4]:
        targets.append(rows.at[begin : begin + source.shape[0]])
        begin += source.shape[0]
    copies = [
        pltpu.make_async_copy(source, target, arrived.at[number])
        for number, (source, target) in enumerate(zip(sources, targets + list(held)))
    ]
    for copy in copies:
        copy.start()
    side = lax.axis_index("groups")
    core, line, floor = places()
    rings = lax.axis_size("tok") // 4
    count = sources[0].shape[0]
    for copy in copies[:4]:
        copy.wait()
    begin = 0
    for number, size in enumerate(sizes):
        pieces = held[begin : begin + size]
        for piece in range(begin, begin + size):
            copies[4 + piece].wait()
        begin += size
        values = pair_product(side, rows, pieces)
        for part in range(2):
            block = lax.rem(floor - first - number + rings, rings) * 4
            block = block + (line ^ part) * 2 + core
            key = block < KV_HEADS
            lanes = pl.ds(pl.multiple_of(block * LM_HEAD, LM_HEAD), LM_HEAD)
            shifted = values[: 2 * count, part * LM_HEAD : (part + 1) * LM_HEAD] + bias[:, lanes]
            turning = jnp.where(key, cosine[...], 1.0)
            cross = jnp.where(key, sine[...], 0.0)
            turned = shifted * turning + pltpu.roll(shifted, LM_HEAD // 2, 1) * cross
            turned = turned.astype(jnp.bfloat16)
            out_own[2 * number + part] = turned[:count]
            out_other[2 * number + part] = turned[count:]
        placed = jnp.dot(
            place[...],
            values[2 * count :].astype(jnp.bfloat16),
            preferred_element_type=jnp.float32,
        )
        out_image[:, number * 2 * LM_HEAD : (number + 1) * 2 * LM_HEAD] = placed.astype(
            jnp.bfloat16
        )


def text_cache_body(*refs):
    pieces, out = refs[:-1], refs[-1]
    core, line, floor = places()
    rings = lax.axis_size("tok") // 4
    for parity, stacks in ((core, pieces[: len(pieces) // 2]), (1 - core, pieces[len(pieces) // 2 :])):
        number = 0
        for stack in stacks:
            for index in range(stack.shape[0]):
                block = lax.rem(floor - number // 2 + rings, rings) * 4
                block = block + (line ^ (number % 2)) * 2 + parity
                begin = pl.multiple_of(block * LM_HEAD, LM_HEAD)
                out[:, pl.ds(begin, LM_HEAD)] = stack[index]
                number += 1


def image_cache_body(*refs, orders):
    arrivals, (bias, cosine, sine, out) = refs[:-4], refs[-4:]
    device_count = arrivals[0].shape[0]
    depth = arrivals[0].shape[1]
    for source in range(device_count):
        rows = slice(source // 2 * depth, (source // 2 + 1) * depth)
        place = 0
        for arrival in arrivals:
            for part in range(arrival.shape[2] // LM_HEAD):
                block = orders[source][place]
                place += 1
                lanes = slice(block * LM_HEAD, (block + 1) * LM_HEAD)
                shifted = (
                    arrival[source, :, part * LM_HEAD : (part + 1) * LM_HEAD].astype(jnp.float32)
                    + bias[:, lanes]
                )
                if block < KV_HEADS:
                    shifted = (
                        shifted * cosine[rows]
                        + pltpu.roll(shifted, LM_HEAD // 2, 1) * sine[rows]
                    )
                out[rows, lanes] = shifted.astype(jnp.bfloat16)


def full_tables(positions):
    half_size = LM_HEAD // 2
    lane = jnp.arange(LM_HEAD, dtype=jnp.int32)
    index_pair = lane % half_size
    frequency = jnp.power(jnp.float32(rope_base), -2.0 * index_pair.astype(jnp.float32) / LM_HEAD)
    section = (index_pair >= half_size // 4).astype(jnp.int32) + (
        index_pair >= half_size // 4 + 3 * half_size // 8
    ).astype(jnp.int32)
    places = positions.astype(jnp.float32)
    chosen = jnp.zeros((positions.shape[1], LM_HEAD), jnp.float32)
    for axis_number in range(3):
        chosen = (
            chosen
            + places[axis_number][:, None] * (section == axis_number).astype(jnp.float32)[None, :]
        )
    angles = chosen * frequency[None, :]
    sign = jnp.where(lane < half_size, -1.0, 1.0)
    return jnp.cos(angles), jnp.sin(angles) * sign[None, :]


def per_device(*args):
    return permuted(*args)


def permuted(
    vis_query,
    vis_keyvalue,
    vis_residual,
    vis_out_weight,
    vis_out_bias,
    image_units,
    text_embed,
    lm_gain,
    lm_kv_weight,
    lm_kv_bias,
    text_positions,
    image_destination,
    image_positions,
):
    bf16, f32 = jnp.bfloat16, jnp.float32
    patch_count, vis_width = vis_query.shape
    head_size = vis_width // VIS_HEADS
    half_window = patch_count // 2
    count = lax.axis_size("tok")
    rings = count // 4
    side = lax.axis_index("groups")
    text_count, lm_width = text_embed.shape
    units = image_destination.shape[0]
    slot_count = image_positions.shape[1]
    capacity = slot_count // count

    def send(value, pairs, axis="tok"):
        return lax.ppermute(value, axis, pairs)

    sibling = [(i, i ^ 1) for i in range(count)]
    across = [(i, i ^ 2) for i in range(count)]
    upward = [(i, (i + 4) % count) for i in range(count)]
    peer = [(0, 1), (1, 0)]

    half_depth = lm_width // 2
    half = lax.dynamic_slice_in_dim(lm_kv_weight, side * half_depth, half_depth, 0)
    ring_halves = [half]
    for _ in range(1, rings):
        ring_halves.append(send(ring_halves[-1], upward))
    whole_across = send(lm_kv_weight, across)
    groups = [[lm_kv_weight, whole_across]]
    for step in range(1, rings):
        mine = [ring_halves[step], send(ring_halves[step], across)]
        peers = [send(mine[0], peer, "groups"), send(mine[1], peer, "groups")]
        groups.append(mine + peers)

    forward = [(i, i + 1) for i in range(count - 1)]
    backward = [(i + 1, i) for i in range(count - 1)]
    low = send(vis_keyvalue[:, patch_count - half_window :], forward)
    high = send(vis_keyvalue[:, :half_window], backward)

    rows_across = send(vis_out_weight, across)
    row_pair = jnp.stack([vis_out_weight, rows_across])
    row_mine = [row_pair]
    for _ in range(1, rings):
        row_mine.append(send(row_mine[-1], upward))
    row_other = [send(piece, sibling) for piece in row_mine]

    target = image_destination[:, 0]
    numbers = jnp.concatenate([text_positions, target])
    other_numbers = send(numbers, sibling)

    gain = lm_gain[None, :]
    normed_own = call_kernel(
        norm_body,
        jax.ShapeDtypeStruct((text_count, lm_width), bf16),
        text_embed,
        gain,
        cost=(text_count * lm_width * 8, 4 * text_count * lm_width),
    )
    normed_other = send(normed_own, sibling)

    attended = []
    wide = vis_width // 2
    for part in range(2):
        column = functools.partial(lambda part, i: (0, part), part)
        deep = functools.partial(lambda part, i: (0, 0, part), part)
        attended.append(
            call_kernel(
                functools.partial(attention_body, head_size=head_size, window=2 * LM_HEAD),
                jax.ShapeDtypeStruct((patch_count, wide), bf16),
                vis_query,
                vis_keyvalue,
                low,
                high,
                image_units[None, :],
                specs=[
                    pl.BlockSpec((patch_count, wide), column),
                    pl.BlockSpec((2, patch_count, wide), deep),
                    pl.BlockSpec((2, half_window, wide), deep),
                    pl.BlockSpec((2, half_window, wide), deep),
                    pl.BlockSpec(memory_space=pltpu.VMEM),
                ],
                cost=(patch_count * patch_count * vis_width * 12, 4 * patch_count * vis_width),
            )
        )

    depth = vis_out_weight.shape[0]
    core, _, _ = places()
    normed_image = call_kernel(
        hidden_body,
        jax.ShapeDtypeStruct((patch_count // 4, 4 * vis_width), bf16),
        *attended,
        *row_mine,
        *row_other,
        vis_out_bias[None, :],
        vis_residual,
        gain,
        scratch=[
            pltpu.VMEM((count * depth, vis_width), bf16),
            pltpu.VMEM((vis_width // LM_HEAD, patch_count, LM_HEAD), f32),
        ],
        cost=(2 * patch_count * vis_width * vis_width, 2 * vis_width * vis_width),
    )
    image_other = send(normed_image, sibling)

    other_target = other_numbers[text_count:]
    slot_own = target * (2 * capacity) + core * capacity + ranks_of(target)
    slot_other = other_target * (2 * capacity) + (1 - core) * capacity + ranks_of(other_target)
    slots = jnp.concatenate([slot_own, slot_other])
    place = (
        jnp.arange(2 * slot_count, dtype=jnp.int32)[:, None] == slots[None, :]
    ).astype(bf16)

    both_positions = jnp.concatenate([text_positions, other_numbers[:text_count]])
    cosine, sine = full_tables(jnp.broadcast_to(both_positions[None, :], (3, 2 * text_count)))
    bias = lm_kv_bias[None, :]

    blocks_own, blocks_other, arrivals = [], [], []
    for number, chosen in enumerate((groups[:-1], groups[-1:])):
        blocks = 2 * len(chosen)
        sources = [normed_own, normed_other, normed_image, image_other]
        sources += [piece for group in chosen for piece in group]
        whole = pl.BlockSpec(memory_space=pltpu.VMEM)
        kept, given, outgoing = call_kernel(
            functools.partial(
                project_body,
                sizes=[len(group) for group in chosen],
                first=0 if number == 0 else rings - 1,
            ),
            [jax.ShapeDtypeStruct((blocks, text_count, LM_HEAD), bf16)] * 2
            + [jax.ShapeDtypeStruct((2 * slot_count, blocks * LM_HEAD), bf16)],
            *sources,
            bias,
            cosine,
            sine,
            place,
            specs=[pl.BlockSpec(memory_space=pl.ANY)] * len(sources) + [whole] * 4,
            scratch=[pltpu.VMEM((2 * (text_count + units), lm_width), bf16)]
            + [pltpu.VMEM(source.shape, bf16) for source in sources[4:]]
            + [pltpu.SemaphoreType.DMA((len(sources),))],
            limit=24,
            cost=(
                4 * (text_count + units) * lm_width * LM_HEAD * blocks,
                4 * text_count * lm_width + 2 * lm_width * LM_HEAD * blocks,
            ),
        )
        blocks_own.append(kept)
        blocks_other.append(send(given, sibling))
        arrived = lax.all_to_all(outgoing, "tok", split_axis=0, concat_axis=0, tiled=True)
        arrivals.append(arrived.reshape(count, 2 * capacity, -1))

    text_cache = call_kernel(
        text_cache_body,
        jax.ShapeDtypeStruct((text_count, count * LM_HEAD), bf16),
        *blocks_own,
        *blocks_other,
    )
    orders = [
        [
            (source // 4 - step) % rings * 4 + (source // 2 % 2 ^ part) * 2 + source % 2
            for step in range(rings)
            for part in range(2)
        ]
        for source in range(count)
    ]
    image_cosine, image_sine = full_tables(image_positions)
    image_cache = call_kernel(
        functools.partial(image_cache_body, orders=orders),
        jax.ShapeDtypeStruct((slot_count, count * LM_HEAD), bf16),
        *arrivals,
        bias,
        image_cosine,
        image_sine,
    )
    return (text_cache, image_cache)


def fits(mesh, args):
    count = mesh.shape["tok"]
    weight = (args[8].shape[0], args[8].shape[1] // count)
    return (
        weight[1] == LM_HEAD
        and mesh.shape["groups"] == 2
        and count % 4 == 0
        and weight[0] % (2 * LM_HEAD) == 0
        and args[3].shape[0] // count % 16 == 0
        and args[12].shape[1] // (2 * count * count) % 8 == 0
    )


def solution(mesh):
    placed = (
        P(("groups", "tok"), None),
        P(None, ("groups", "tok"), None),
        P(("groups", "tok"), None),
        P("tok", None),
        P(),
        P("groups"),
        P(("groups", "tok"), None),
        P(),
        P(None, "tok"),
        P(),
        P(("groups", "tok")),
        P(("groups", "tok"), None),
        P(None, ("groups", "tok")),
    )

    specs = (P(("groups", "tok"), None), P(("groups", "tok"), None))

    def mapped(body):
        return jax.shard_map(
            body, mesh=mesh, in_specs=placed, out_specs=specs, check_vma=False
        )

    def chosen(*args):
        return mapped(per_device if fits(mesh, args) else per_device_gathered)(*args)

    return chosen
```

profile of v0, /device:TPU:0, one launch (start us, length us, event | category | flops | bytes accessed | tf_op | source)
XLA Modules:
  0.0 188.4 jit_solution(12038103961226750824)
XLA Ops:
  0.7 3.1 %collective-permute-start.3 = (bf16[80,1280]{1,0:T(8,128)(2,1)}, bf16[80,1280]{1,0:T(8,128)(2,1)S(1)}, u32[]{:S(2)}, u32[]{:S(2)}) collective-permute-start(bf16[80,1280]{1,0:T(8,128)(2,1)} %param.16), channel_id=1, source_target_pairs={{0,2},{1,3},{2,0},{3,1},{4,6},{5,7},{6,4},{7,5},{8,10},{9,11},{10,... | collective-permute-start | bytes 614408 | tf_op jit(solution)/shard_map/ppermute | solution.py:455
  3.7 2.4 %fusion.8 = (bf16[2,128,1280]{2,1,0:T(8,128)(2,1)}, bf16[2,128,1280]{2,1,0:T(8,128)(2,1)}) fusion(bf16[2,256,1280]{2,1,0:T(8,128)(2,1)} %own.3), kind=kLoop, calls=%fused_computation.34 | loop fusion | bytes 2621440 | tf_op jit(solution)/shard_map/slice | solution.py:477
  6.2 2.4 %collective-permute-start.1 = (bf16[2,128,1280]{2,1,0:T(8,128)(2,1)}, bf16[2,128,1280]{2,1,0:T(8,128)(2,1)}, u32[]{:S(2)}, u32[]{:S(2)}) collective-permute-start(bf16[2,128,1280]{2,1,0:T(8,128)(2,1)} %get-tuple-element.15), channel_id=1, source_target_pairs={{0,1},{1,2},{2,3},{3,4},{4,5},{5,6},{6,7},{7,8},{8,9},{9,10},{10,1... | collective-permute-start | bytes 1966088 | tf_op jit(solution)/shard_map/ppermute | solution.py:455
  8.6 1.3 collective-permute-start.2
  9.9 2.1 %collective-permute-start.12 = (bf16[5120,128]{1,0:T(8,128)(2,1)}, bf16[5120,128]{1,0:T(8,128)(2,1)}, u32[]{:S(2)}, u32[]{:S(2)}) collective-permute-start(bf16[5120,128]{1,0:T(8,128)(2,1)} %refs_4_.1), channel_id=1, source_target_pairs={{0,2},{1,3},{2,0},{3,1},{4,6},{5,7},{6,4},{7,5},{8,10},{9,11},{10,... | collective-permute-start | bytes 3932168 | tf_op jit(solution)/shard_map/ppermute | solution.py:455
  12.0 2.5 %collective-permute-start.4 = (bf16[2,80,1280]{2,1,0:T(8,128)(2,1)S(1)}, bf16[2,80,1280]{2,1,0:T(8,128)(2,1)S(1)}, u32[]{:S(2)}, u32[]{:S(2)}) collective-permute-start(bf16[2,80,1280]{2,1,0:T(8,128)(2,1)S(1)} %pad_maximum_fusion.refs_0_), channel_id=1, source_target_pairs={{0,4},{1,5},{2,6},{3,7},{4,8},{5,9},{6,10},{7,11},{8,12},{9,13},{1... | collective-permute-start | bytes 1228808 | tf_op jit(solution)/shard_map/ppermute | solution.py:455
  14.7 1.1 collective-permute-done.21
  16.0 1.1 constant_dynamic-slice_fusion
  17.1 19.7 %collective-permute-done.4.refs_1_ = bf16[2,80,1280]{2,1,0:T(8,128)(2,1)S(1)} collective-permute-done((bf16[2,80,1280]{2,1,0:T(8,128)(2,1)S(1)}, bf16[2,80,1280]{2,1,0:T(8,128)(2,1)S(1)}, u32[]{:S(2)}, u32[]{:S(2)}) %collective-permute-start.4) | collective-permute-done | bytes 409632 | tf_op jit(solution)/shard_map/ppermute | solution.py:455
  36.8 0.8 copy-done.11
  37.6 1.7 copy-done
  39.4 1.5 shard_map.140.refs_0_
  41.4 18.9 %collective-permute-done.5.refs_2_ = bf16[2,80,1280]{2,1,0:T(8,128)(2,1)S(1)} collective-permute-done((bf16[2,80,1280]{2,1,0:T(8,128)(2,1)S(1)}, bf16[2,80,1280]{2,1,0:T(8,128)(2,1)S(1)}, u32[]{:S(2)}, u32[]{:S(2)}) %collective-permute-start.5) | collective-permute-done | bytes 409632 | tf_op jit(solution)/shard_map/ppermute | solution.py:455
  60.5 0.8 copy-done.15
  61.3 10.9 %collective-permute-done.6.refs_3_ = bf16[2,80,1280]{2,1,0:T(8,128)(2,1)} collective-permute-done((bf16[2,80,1280]{2,1,0:T(8,128)(2,1)S(1)}, bf16[2,80,1280]{2,1,0:T(8,128)(2,1)}, u32[]{:S(2)}, u32[]{:S(2)}) %collective-permute-start.6) | collective-permute-done | bytes 409632 | tf_op jit(solution)/shard_map/ppermute | solution.py:455
  72.9 1.6 collective-permute-start.15
  74.5 4.7 %collective-permute-done.17.refs_10_ = bf16[2560,128]{1,0:T(8,128)(2,1)} collective-permute-done((bf16[2560,128]{1,0:T(8,128)(2,1)}, bf16[2560,128]{1,0:T(8,128)(2,1)}, u32[]{:S(2)}, u32[]{:S(2)}) %collective-permute-start.17) | collective-permute-done | bytes 655392 | tf_op jit(solution)/shard_map/ppermute | solution.py:455
  79.2 3.2 %collective-permute-start.18 = (bf16[2560,128]{1,0:T(8,128)(2,1)}, bf16[2560,128]{1,0:T(8,128)(2,1)}, u32[]{:S(2)}, u32[]{:S(2)}) collective-permute-start(bf16[2560,128]{1,0:T(8,128)(2,1)} %collective-permute-done.17.refs_10_), channel_id=1, source_target_pairs={{0,2},{1,3},{2,0},{3,1},{4,6},{5,7},{6,4},{7,5},{8,10},{9,11},{10,... | collective-permute-start | bytes 1966088 | tf_op jit(solution)/shard_map/ppermute | solution.py:455
  82.4 0.8 copy-done.19
  83.3 1.5 collective-permute-start.16
  85.0 1.3 copy-done.3
  86.3 1.1 copy-done.31
  87.4 6.7 %shard_map.141.first = bf16[256,640]{1,0:T(8,128)(2,1)S(1)} custom-call(bf16[256,1280]{1,0:T(8,128)(2,1)S(1)} %copy-done.31, bf16[2,256,1280]{2,1,0:T(8,128)(2,1)S(1)} %copy-done.3, bf16[2,128,1280]{2,1,0:T(8,128)(2,1)} %collective-permute-done.1.low, bf16[2,128,1280]{2,1,0:T(8,128)(2,1)} %collective-permute-done.2.high, s32[1,48]{1,0:T(1,128)S(1)} %bitcast.22), custom_call_target="tpu_custom_call" | custom-call | flops 1006632960 | bytes 1310720 | tf_op jit(solution)/shard_map/pallas_call | solution.py:182
  94.2 6.8 %shard_map.142.second = bf16[256,640]{1,0:T(8,128)(2,1)S(1)} custom-call(bf16[256,1280]{1,0:T(8,128)(2,1)S(1)} %copy-done.32, bf16[2,256,1280]{2,1,0:T(8,128)(2,1)S(1)} %copy-done.3, bf16[2,128,1280]{2,1,0:T(8,128)(2,1)} %collective-permute-done.1.low, bf16[2,128,1280]{2,1,0:T(8,128)(2,1)} %collective-permute-done.2.high, s32[1,48]{1,0:T(1,128)S(1)} %bitcast.23), custom_call_target="tpu_custom_call" | custom-call | flops 1006632960 | bytes 1310720 | tf_op jit(solution)/shard_map/pallas_call | solution.py:182
  101.0 1.0 copy-done.14
  102.0 1.0 copy-done.18
  103.0 2.7 %shard_map.143.refs_2_ = bf16[64,5120]{1,0:T(8,128)(2,1)S(1)} custom-call(bf16[256,640]{1,0:T(8,128)(2,1)S(1)} %shard_map.141.first, bf16[256,640]{1,0:T(8,128)(2,1)S(1)} %shard_map.142.second, bf16[2,80,1280]{2,1,0:T(8,128)(2,1)S(1)} %copy-done.2, bf16[2,80,1280]{2,1,0:T(8,128)(2,1)S(1)} %copy-done.10, bf16[2,80,1280]{2,1,0:T(8,128)(2,1)S(1)} %copy-done.14, ...), custom_call_target="tpu_custom_call" | custom-call | flops 838860800 | bytes 3276800 | tf_op jit(solution)/shard_map/pallas_call | solution.py:182
  106.3 1.6 collective-permute-start.20
  108.2 1.0 fusion.2
  109.3 14.4 %collective-permute-done.19.refs_12_ = bf16[2560,128]{1,0:T(8,128)(2,1)S(1)} collective-permute-done((bf16[2560,128]{1,0:T(8,128)(2,1)}, bf16[2560,128]{1,0:T(8,128)(2,1)S(1)}, u32[]{:S(2)}, u32[]{:S(2)}) %collective-permute-start.19) | collective-permute-done | bytes 655392 | tf_op jit(solution)/shard_map/ppermute | solution.py:455
  124.2 0.9 collective-permute-done.23.refs_5_
  125.7 12.0 %collective-permute-done.20.refs_13_ = bf16[2560,128]{1,0:T(8,128)(2,1)S(1)} collective-permute-done((bf16[2560,128]{1,0:T(8,128)(2,1)}, bf16[2560,128]{1,0:T(8,128)(2,1)S(1)}, u32[]{:S(2)}, u32[]{:S(2)}) %collective-permute-start.20) | collective-permute-done | bytes 655392 | tf_op jit(solution)/shard_map/ppermute | solution.py:455
  137.7 12.4 %shard_map.144 = (bf16[6,256,128]{2,1,0:T(8,128)(2,1)S(1)}, bf16[6,256,128]{2,1,0:T(8,128)(2,1)S(1)}, bf16[256,768]{1,0:T(8,128)(2,1)S(1)}) custom-call(bf16[256,5120]{1,0:T(8,128)(2,1)S(1)} %shard_map.140.refs_0_, bf16[256,5120]{1,0:T(8,128)(2,1)} %collective-permute-done.refs_1_, bf16[64,5120]{1,0:T(8,128)(2,1)S(1)} %shard_map.143.refs_2_, ...), custom_call_target="tpu_custom_call" | custom-call | flops 5033164800 | bytes 13107200 | tf_op jit(solution)/shard_map/pallas_call | solution.py:182
  150.9 0.8 copy-done.23
  151.6 0.8 copy-done.33
  152.4 5.2 %all-to-all-start = ((bf16[16,16,768]{2,1,0:T(8,128)(2,1)}), bf16[16,16,768]{2,1,0:T(8,128)(2,1)}, u32[]{:S(2)}, u32[]{:S(2)}) async-start(bf16[16,16,768]{2,1,0:T(8,128)(2,1)} %bitcast.15), calls=%async_computation | async-start | bytes 786432 | tf_op jit(solution)/shard_map/all_to_all | solution.py:587
  159.8 4.1 %collective-permute-done.25.refs_7_ = bf16[2560,128]{1,0:T(8,128)(2,1)} collective-permute-done((bf16[2560,128]{1,0:T(8,128)(2,1)}, bf16[2560,128]{1,0:T(8,128)(2,1)}, u32[]{:S(2)}, u32[]{:S(2)}) %collective-permute-start.25) | collective-permute-done | bytes 655392 | tf_op jit(solution)/shard_map/ppermute | solution.py:455
  163.9 0.9 copy-done.5
  164.8 1.1 copy-done.7
  165.9 0.8 copy-done.25
  166.8 4.9 %shard_map.145 = (bf16[2,256,128]{2,1,0:T(8,128)(2,1)S(1)}, bf16[2,256,128]{2,1,0:T(8,128)(2,1)S(1)}, bf16[256,256]{1,0:T(8,128)(2,1)S(1)}) custom-call(bf16[256,5120]{1,0:T(8,128)(2,1)S(1)} %shard_map.140.refs_0_, bf16[256,5120]{1,0:T(8,128)(2,1)} %collective-permute-done.refs_1_, bf16[64,5120]{1,0:T(8,128)(2,1)S(1)} %shard_map.143.refs_2_, ...), custom_call_target="tpu_custom_call" | custom-call | flops 1677721600 | bytes 7864320 | tf_op jit(solution)/shard_map/pallas_call | solution.py:182
  173.6 4.9 %all-to-all-start.1 = ((bf16[16,16,256]{2,1,0:T(8,128)(2,1)}), bf16[16,16,256]{2,1,0:T(8,128)(2,1)S(1)}, u32[]{:S(2)}, u32[]{:S(2)}) async-start(bf16[16,16,256]{2,1,0:T(8,128)(2,1)} %bitcast.16), calls=%async_computation.1 | async-start | bytes 262144 | tf_op jit(solution)/shard_map/all_to_all | solution.py:587
  179.0 1.0 sine_multiply_fusion
  180.2 1.0 copy-done.22
  181.2 0.9 copy-done.27
  182.1 2.3 %shard_map.146 = bf16[256,2048]{1,0:T(8,128)(2,1)} custom-call(bf16[6,256,128]{2,1,0:T(8,128)(2,1)S(1)} %copy-done.22, bf16[2,256,128]{2,1,0:T(8,128)(2,1)S(1)} %copy-done.27, bf16[6,256,128]{2,1,0:T(8,128)(2,1)} %collective-permute-done.26.refs_2_, bf16[2,256,128]{2,1,0:T(8,128)(2,1)S(1)} %collective-permute-done.27.refs_3_), custom_call_target="tpu_custom_call" | custom-call | tf_op jit(solution)/shard_map/pallas_call | solution.py:182
  184.4 2.1 %all-to-all-done.1.refs_1_ = bf16[16,16,256]{2,1,0:T(8,128)(2,1)S(1)} async-done(((bf16[16,16,256]{2,1,0:T(8,128)(2,1)}), bf16[16,16,256]{2,1,0:T(8,128)(2,1)S(1)}, u32[]{:S(2)}, u32[]{:S(2)}) %all-to-all-start.1) | async-done | bytes 131104 | tf_op jit(solution)/shard_map/all_to_all | solution.py:587
  186.4 2.0 %shard_map.147 = bf16[128,2048]{1,0:T(8,128)(2,1)} custom-call(bf16[16,16,768]{2,1,0:T(8,128)(2,1)} %all-to-all-done.refs_0_, bf16[16,16,256]{2,1,0:T(8,128)(2,1)S(1)} %all-to-all-done.1.refs_1_, f32[1,2048]{1,0:T(1,128)S(1)} %bitcast.21, f32[128,128]{1,0:T(8,128)S(1)} %get-tuple-element.17.refs_3_, f32[128,128]{1,0:T(8,128)S(1)} %get-tuple-element.16.refs_4_), custom_call_target="tpu_custom_call" | custom-call | tf_op jit(solution)/shard_map/pallas_call | solution.py:182
  (127 shorter events, 9.6 us)
Async XLA Ops:
  0.6 11.3 %copy-start.36 = (bf16[80,1280]{1,0:T(8,128)(2,1)S(1)}, bf16[80,1280]{1,0:T(8,128)(2,1)}, u32[]{:S(2)}) copy-start(bf16[80,1280]{1,0:T(8,128)(2,1)} %param.16) | copy-start | bytes 614404
  0.6 13.9 %copy-start.40 = (s32[64,1]{0,1:T(1,128)S(1)}, s32[64,1]{0,1:T(1,128)}, u32[]{:S(2)}) copy-start(s32[64,1]{0,1:T(1,128)} %param.24) | copy-start | bytes 772
  0.7 13.9 %copy-start.38 = (s32[256]{0:T(256)S(1)}, s32[256]{0:T(256)}, u32[]{:S(2)}) copy-start(s32[256]{0:T(256)} %param.23) | copy-start | bytes 3076
  0.7 11.3 %collective-permute-start.3 = (bf16[80,1280]{1,0:T(8,128)(2,1)}, bf16[80,1280]{1,0:T(8,128)(2,1)S(1)}, u32[]{:S(2)}, u32[]{:S(2)}) collective-permute-start(bf16[80,1280]{1,0:T(8,128)(2,1)} %param.16), channel_id=1, source_target_pairs={{0,2},{1,3},{2,0},{3,1},{4,6},{5,7},{6,4},{7,5},{8,10},{9,11},{10,... | collective-permute-start | bytes 614408 | tf_op jit(solution)/shard_map/ppermute | solution.py:455
  6.2 31.4 %copy-start.29 = (f32[5120]{0:T(1024)S(1)}, f32[5120]{0:T(1024)}, u32[]{:S(2)}) copy-start(f32[5120]{0:T(1024)} %param.20) | copy-start | bytes 61444
  6.2 34.7 %collective-permute-start.1 = (bf16[2,128,1280]{2,1,0:T(8,128)(2,1)}, bf16[2,128,1280]{2,1,0:T(8,128)(2,1)}, u32[]{:S(2)}, u32[]{:S(2)}) collective-permute-start(bf16[2,128,1280]{2,1,0:T(8,128)(2,1)} %get-tuple-element.15), channel_id=1, source_target_pairs={{0,1},{1,2},{2,3},{3,4},{4,5},{5,6},{6,7},{7,8},{8,9},{9,10},{10,1... | collective-permute-start | bytes 1966088 | tf_op jit(solution)/shard_map/ppermute | solution.py:455
  8.6 32.3 %collective-permute-start.2 = (bf16[2,128,1280]{2,1,0:T(8,128)(2,1)}, bf16[2,128,1280]{2,1,0:T(8,128)(2,1)}, u32[]{:S(2)}, u32[]{:S(2)}) collective-permute-start(bf16[2,128,1280]{2,1,0:T(8,128)(2,1)} %get-tuple-element.14), channel_id=1, source_target_pairs={{1,0},{2,1},{3,2},{4,3},{5,4},{6,5},{7,6},{8,7},{9,8},{10,9},{11,1... | collective-permute-start | bytes 1966088 | tf_op jit(solution)/shard_map/ppermute | solution.py:455
  9.9 51.4 %collective-permute-start.12 = (bf16[5120,128]{1,0:T(8,128)(2,1)}, bf16[5120,128]{1,0:T(8,128)(2,1)}, u32[]{:S(2)}, u32[]{:S(2)}) collective-permute-start(bf16[5120,128]{1,0:T(8,128)(2,1)} %refs_4_.1), channel_id=1, source_target_pairs={{0,2},{1,3},{2,0},{3,1},{4,6},{5,7},{6,4},{7,5},{8,10},{9,11},{10,... | collective-permute-start | bytes 3932168 | tf_op jit(solution)/shard_map/ppermute | solution.py:455
  12.0 25.6 %copy-start.1 = (bf16[2,80,1280]{2,1,0:T(8,128)(2,1)}, bf16[2,80,1280]{2,1,0:T(8,128)(2,1)S(1)}, u32[]{:S(2)}) copy-start(bf16[2,80,1280]{2,1,0:T(8,128)(2,1)S(1)} %pad_maximum_fusion.refs_0_) | copy-start | bytes 1228804
  12.0 24.8 %collective-permute-start.4 = (bf16[2,80,1280]{2,1,0:T(8,128)(2,1)S(1)}, bf16[2,80,1280]{2,1,0:T(8,128)(2,1)S(1)}, u32[]{:S(2)}, u32[]{:S(2)}) collective-permute-start(bf16[2,80,1280]{2,1,0:T(8,128)(2,1)S(1)} %pad_maximum_fusion.refs_0_), channel_id=1, source_target_pairs={{0,4},{1,5},{2,6},{3,7},{4,8},{5,9},{6,10},{7,11},{8,12},{9,13},{1... | collective-permute-start | bytes 1228808 | tf_op jit(solution)/shard_map/ppermute | solution.py:455
  14.6 1.2 collective-permute-start.21
  15.8 69.2 %copy-start.39 = (s32[320]{0:T(512)}, s32[320]{0:T(512)S(1)}, u32[]{:S(2)}) copy-start(s32[320]{0:T(512)S(1)} %collective-permute-done.21) | copy-start | bytes 3844
  15.8 21.0 %collective-permute-start.7 = (bf16[2,80,1280]{2,1,0:T(8,128)(2,1)S(1)}, bf16[2,80,1280]{2,1,0:T(8,128)(2,1)S(1)}, u32[]{:S(2)}, u32[]{:S(2)}) collective-permute-start(bf16[2,80,1280]{2,1,0:T(8,128)(2,1)S(1)} %pad_maximum_fusion.refs_0_), channel_id=1, source_target_pairs={{0,1},{1,0},{2,3},{3,2},{4,5},{5,4},{6,7},{7,6},{8,9},{9,8},{10,11... | collective-permute-start | bytes 1228808 | tf_op jit(solution)/shard_map/ppermute | solution.py:455
  36.8 23.6 %collective-permute-start.13 = (bf16[2560,128]{1,0:T(8,128)(2,1)S(1)}, bf16[2560,128]{1,0:T(8,128)(2,1)}, u32[]{:S(2)}, u32[]{:S(2)}) collective-permute-start(bf16[2560,128]{1,0:T(8,128)(2,1)S(1)} %constant_dynamic-slice_fusion), channel_id=1, source_target_pairs={{0,4},{1,5},{2,6},{3,7},{4,8},{5,9},{6,10},{7,11},{8,12},{9,13},{1... | collective-permute-start | bytes 1966088 | tf_op jit(solution)/shard_map/ppermute | solution.py:455
  37.6 22.8 %collective-permute-start.5 = (bf16[2,80,1280]{2,1,0:T(8,128)(2,1)S(1)}, bf16[2,80,1280]{2,1,0:T(8,128)(2,1)S(1)}, u32[]{:S(2)}, u32[]{:S(2)}) collective-permute-start(bf16[2,80,1280]{2,1,0:T(8,128)(2,1)S(1)} %collective-permute-done.4.refs_1_), channel_id=1, source_target_pairs={{0,4},{1,5},{2,6},{3,7},{4,8},{5,9},{6,10},{7,11},{8,12},{9,13},{1... | collective-permute-start | bytes 1228808 | tf_op jit(solution)/shard_map/ppermute | solution.py:455
  39.4 45.4 %copy-start.37 = (f32[1280]{0:T(1024)S(1)}, f32[1280]{0:T(1024)}, u32[]{:S(2)}) copy-start(f32[1280]{0:T(1024)} %param.17) | copy-start | bytes 15364
  39.4 45.6 %copy-start.35 = (s32[48]{0:T(128)S(1)}, s32[48]{0:T(128)}, u32[]{:S(2)}) copy-start(s32[48]{0:T(128)} %param.18) | copy-start | bytes 580
  40.8 84.8 %collective-permute-start = (bf16[256,5120]{1,0:T(8,128)(2,1)S(1)}, bf16[256,5120]{1,0:T(8,128)(2,1)}, u32[]{:S(2)}, u32[]{:S(2)}) collective-permute-start(bf16[256,5120]{1,0:T(8,128)(2,1)S(1)} %shard_map.140.refs_0_), channel_id=1, source_target_pairs={{0,1},{1,0},{2,3},{3,2},{4,5},{5,4},{6,7},{7,6},{8,9},{9,8},{10,11... | collective-permute-start | bytes 7864328 | tf_op jit(solution)/shard_map/ppermute | solution.py:455
  40.9 19.5 %collective-permute-start.8 = (bf16[2,80,1280]{2,1,0:T(8,128)(2,1)S(1)}, bf16[2,80,1280]{2,1,0:T(8,128)(2,1)S(1)}, u32[]{:S(2)}, u32[]{:S(2)}) collective-permute-start(bf16[2,80,1280]{2,1,0:T(8,128)(2,1)S(1)} %collective-permute-done.4.refs_1_), channel_id=1, source_target_pairs={{0,1},{1,0},{2,3},{3,2},{4,5},{5,4},{6,7},{7,6},{8,9},{9,8},{10,11... | collective-permute-start | bytes 1228808 | tf_op jit(solution)/shard_map/ppermute | solution.py:455
  60.4 33.7 %copy-start.13 = (bf16[2,80,1280]{2,1,0:T(8,128)(2,1)}, bf16[2,80,1280]{2,1,0:T(8,128)(2,1)S(1)}, u32[]{:S(2)}) copy-start(bf16[2,80,1280]{2,1,0:T(8,128)(2,1)S(1)} %collective-permute-done.5.refs_2_) | copy-start | bytes 1228804
  60.4 11.8 %collective-permute-start.6 = (bf16[2,80,1280]{2,1,0:T(8,128)(2,1)S(1)}, bf16[2,80,1280]{2,1,0:T(8,128)(2,1)}, u32[]{:S(2)}, u32[]{:S(2)}) collective-permute-start(bf16[2,80,1280]{2,1,0:T(8,128)(2,1)S(1)} %collective-permute-done.5.refs_2_), channel_id=1, source_target_pairs={{0,4},{1,5},{2,6},{3,7},{4,8},{5,9},{6,10},{7,11},{8,12},{9,13},{1... | collective-permute-start | bytes 1228808 | tf_op jit(solution)/shard_map/ppermute | solution.py:455
  60.4 12.5 %collective-permute-start.14 = (bf16[2560,128]{1,0:T(8,128)(2,1)}, bf16[2560,128]{1,0:T(8,128)(2,1)}, u32[]{:S(2)}, u32[]{:S(2)}) collective-permute-start(bf16[2560,128]{1,0:T(8,128)(2,1)} %collective-permute-done.13.refs_6_), channel_id=1, source_target_pairs={{0,2},{1,3},{2,0},{3,1},{4,6},{5,7},{6,4},{7,5},{8,10},{9,11},{10,... | collective-permute-start | bytes 1966088 | tf_op jit(solution)/shard_map/ppermute | solution.py:455
  61.3 17.9 %collective-permute-start.17 = (bf16[2560,128]{1,0:T(8,128)(2,1)}, bf16[2560,128]{1,0:T(8,128)(2,1)}, u32[]{:S(2)}, u32[]{:S(2)}) collective-permute-start(bf16[2560,128]{1,0:T(8,128)(2,1)} %collective-permute-done.13.refs_6_), channel_id=1, source_target_pairs={{0,4},{1,5},{2,6},{3,7},{4,8},{5,9},{6,10},{7,11},{8,12},{9,13},{1... | collective-permute-start | bytes 1966088 | tf_op jit(solution)/shard_map/ppermute | solution.py:455
  61.3 21.1 %collective-permute-start.9 = (bf16[2,80,1280]{2,1,0:T(8,128)(2,1)S(1)}, bf16[2,80,1280]{2,1,0:T(8,128)(2,1)S(1)}, u32[]{:S(2)}, u32[]{:S(2)}) collective-permute-start(bf16[2,80,1280]{2,1,0:T(8,128)(2,1)S(1)} %collective-permute-done.5.refs_2_), channel_id=1, source_target_pairs={{0,1},{1,0},{2,3},{3,2},{4,5},{5,4},{6,7},{7,6},{8,9},{9,8},{10,11... | collective-permute-start | bytes 1228808 | tf_op jit(solution)/shard_map/ppermute | solution.py:455
  72.2 10.3 %collective-permute-start.10 = (bf16[2,80,1280]{2,1,0:T(8,128)(2,1)}, bf16[2,80,1280]{2,1,0:T(8,128)(2,1)S(1)}, u32[]{:S(2)}, u32[]{:S(2)}) collective-permute-start(bf16[2,80,1280]{2,1,0:T(8,128)(2,1)} %collective-permute-done.6.refs_3_), channel_id=1, source_target_pairs={{0,1},{1,0},{2,3},{3,2},{4,5},{5,4},{6,7},{7,6},{8,9},{9,8},{10,11... | collective-permute-start | bytes 1228808 | tf_op jit(solution)/shard_map/ppermute | solution.py:455
  72.9 32.8 %collective-permute-start.15 = (bf16[2560,128]{1,0:T(8,128)(2,1)}, bf16[2560,128]{1,0:T(8,128)(2,1)}, u32[]{:S(2)}, u32[]{:S(2)}) collective-permute-start(bf16[2560,128]{1,0:T(8,128)(2,1)} %collective-permute-done.13.refs_6_), channel_id=1, source_target_pairs={{0,16},{16,0},{1,17},{17,1},{2,18},{18,2},{3,19},{19,3},{4,20},{20... | collective-permute-start | bytes 1966088 | tf_op jit(solution)/shard_map/ppermute | solution.py:455
  79.2 27.2 %collective-permute-start.18 = (bf16[2560,128]{1,0:T(8,128)(2,1)}, bf16[2560,128]{1,0:T(8,128)(2,1)}, u32[]{:S(2)}, u32[]{:S(2)}) collective-permute-start(bf16[2560,128]{1,0:T(8,128)(2,1)} %collective-permute-done.17.refs_10_), channel_id=1, source_target_pairs={{0,2},{1,3},{2,0},{3,1},{4,6},{5,7},{6,4},{7,5},{8,10},{9,11},{10,... | collective-permute-start | bytes 1966088 | tf_op jit(solution)/shard_map/ppermute | solution.py:455
  82.4 11.7 %copy-start.17 = (bf16[2,80,1280]{2,1,0:T(8,128)(2,1)}, bf16[2,80,1280]{2,1,0:T(8,128)(2,1)S(1)}, u32[]{:S(2)}) copy-start(bf16[2,80,1280]{2,1,0:T(8,128)(2,1)S(1)} %collective-permute-done.9.refs_6_) | copy-start | bytes 1228804
  82.4 25.5 %collective-permute-start.22 = (bf16[2560,128]{1,0:T(8,128)(2,1)}, bf16[2560,128]{1,0:T(8,128)(2,1)}, u32[]{:S(2)}, u32[]{:S(2)}) collective-permute-start(bf16[2560,128]{1,0:T(8,128)(2,1)} %collective-permute-done.17.refs_10_), channel_id=1, source_target_pairs={{0,4},{1,5},{2,6},{3,7},{4,8},{5,9},{6,10},{7,11},{8,12},{9,13},{1... | collective-permute-start | bytes 1966088 | tf_op jit(solution)/shard_map/ppermute | solution.py:455
  83.3 23.1 %collective-permute-start.16 = (bf16[2560,128]{1,0:T(8,128)(2,1)}, bf16[2560,128]{1,0:T(8,128)(2,1)}, u32[]{:S(2)}, u32[]{:S(2)}) collective-permute-start(bf16[2560,128]{1,0:T(8,128)(2,1)} %collective-permute-done.14.refs_7_), channel_id=1, source_target_pairs={{0,16},{16,0},{1,17},{17,1},{2,18},{18,2},{3,19},{19,3},{4,20},{20... | collective-permute-start | bytes 1966088 | tf_op jit(solution)/shard_map/ppermute | solution.py:455
  94.1 6.8 %copy-start.2 = (bf16[2,80,1280]{2,1,0:T(8,128)(2,1)S(1)}, bf16[2,80,1280]{2,1,0:T(8,128)(2,1)}, u32[]{:S(2)}) copy-start(bf16[2,80,1280]{2,1,0:T(8,128)(2,1)} %copy-done.1) | copy-start | bytes 1228804
  94.1 6.8 %copy-start.8 = (bf16[256,1280]{1,0:T(8,128)(2,1)S(1)}, bf16[256,1280]{1,0:T(8,128)(2,1)}, u32[]{:S(2)}) copy-start(bf16[256,1280]{1,0:T(8,128)(2,1)} %refs_9_.1) | copy-start | bytes 1966084
  94.1 6.8 %copy-start.10 = (bf16[2,80,1280]{2,1,0:T(8,128)(2,1)S(1)}, bf16[2,80,1280]{2,1,0:T(8,128)(2,1)}, u32[]{:S(2)}) copy-start(bf16[2,80,1280]{2,1,0:T(8,128)(2,1)} %copy-done.9) | copy-start | bytes 1228804
  94.1 6.8 %copy-start.12 = (bf16[2,80,1280]{2,1,0:T(8,128)(2,1)S(1)}, bf16[2,80,1280]{2,1,0:T(8,128)(2,1)}, u32[]{:S(2)}) copy-start(bf16[2,80,1280]{2,1,0:T(8,128)(2,1)} %copy-done.11) | copy-start | bytes 1228804
  103.0 34.6 %copy-start.30 = (f32[2048]{0:T(1024)S(1)}, f32[2048]{0:T(1024)}, u32[]{:S(2)}) copy-start(f32[2048]{0:T(1024)} %param.22) | copy-start | bytes 24580
  105.7 17.9 %collective-permute-start.19 = (bf16[2560,128]{1,0:T(8,128)(2,1)}, bf16[2560,128]{1,0:T(8,128)(2,1)S(1)}, u32[]{:S(2)}, u32[]{:S(2)}) collective-permute-start(bf16[2560,128]{1,0:T(8,128)(2,1)} %collective-permute-done.17.refs_10_), channel_id=1, source_target_pairs={{0,16},{16,0},{1,17},{17,1},{2,18},{18,2},{3,19},{19,3},{4,20},{20... | collective-permute-start | bytes 1966088 | tf_op jit(solution)/shard_map/ppermute | solution.py:455
  106.3 19.3 %collective-permute-start.11 = (bf16[64,5120]{1,0:T(8,128)(2,1)S(1)}, bf16[64,5120]{1,0:T(8,128)(2,1)S(1)}, u32[]{:S(2)}, u32[]{:S(2)}) collective-permute-start(bf16[64,5120]{1,0:T(8,128)(2,1)S(1)} %shard_map.143.refs_2_), channel_id=1, source_target_pairs={{0,1},{1,0},{2,3},{3,2},{4,5},{5,4},{6,7},{7,6},{8,9},{9,8},{10,11... | collective-permute-start | bytes 1966088 | tf_op jit(solution)/shard_map/ppermute | solution.py:455
  106.3 31.3 %collective-permute-start.20 = (bf16[2560,128]{1,0:T(8,128)(2,1)}, bf16[2560,128]{1,0:T(8,128)(2,1)S(1)}, u32[]{:S(2)}, u32[]{:S(2)}) collective-permute-start(bf16[2560,128]{1,0:T(8,128)(2,1)} %collective-permute-done.18.refs_11_), channel_id=1, source_target_pairs={{0,16},{16,0},{1,17},{17,1},{2,18},{18,2},{3,19},{19,3},{4,20},{20... | collective-permute-start | bytes 1966088 | tf_op jit(solution)/shard_map/ppermute | solution.py:455
  107.9 17.1 %collective-permute-start.23 = (bf16[2560,128]{1,0:T(8,128)(2,1)}, bf16[2560,128]{1,0:T(8,128)(2,1)}, u32[]{:S(2)}, u32[]{:S(2)}) collective-permute-start(bf16[2560,128]{1,0:T(8,128)(2,1)} %collective-permute-done.22.refs_4_), channel_id=1, source_target_pairs={{0,2},{1,3},{2,0},{3,1},{4,6},{5,7},{6,4},{7,5},{8,10},{9,11},{10,... | collective-permute-start | bytes 1966088 | tf_op jit(solution)/shard_map/ppermute | solution.py:455
  108.2 41.9 %copy-start.24 = (bf16[256,128]{1,0:T(8,128)(2,1)}, bf16[256,128]{1,0:T(8,128)(2,1)S(1)}, u32[]{:S(2)}) copy-start(bf16[256,128]{1,0:T(8,128)(2,1)S(1)} %fusion.3.refs_17_.refs_11_) | copy-start | bytes 196612
  109.2 40.9 %copy-start.4 = (f32[512,128]{1,0:T(8,128)}, f32[512,128]{1,0:T(8,128)S(1)}, u32[]{:S(2)}) copy-start(f32[512,128]{1,0:T(8,128)S(1)} %get-tuple-element.19.refs_15_.refs_9_) | copy-start | bytes 786436
  123.6 36.1 %collective-permute-start.24 = (bf16[2560,128]{1,0:T(8,128)(2,1)}, bf16[2560,128]{1,0:T(8,128)(2,1)}, u32[]{:S(2)}, u32[]{:S(2)}) collective-permute-start(bf16[2560,128]{1,0:T(8,128)(2,1)} %collective-permute-done.22.refs_4_), channel_id=1, source_target_pairs={{0,16},{16,0},{1,17},{17,1},{2,18},{18,2},{3,19},{19,3},{4,20},{20... | collective-permute-start | bytes 1966088 | tf_op jit(solution)/shard_map/ppermute | solution.py:455
  125.0 38.9 %collective-permute-start.25 = (bf16[2560,128]{1,0:T(8,128)(2,1)}, bf16[2560,128]{1,0:T(8,128)(2,1)}, u32[]{:S(2)}, u32[]{:S(2)}) collective-permute-start(bf16[2560,128]{1,0:T(8,128)(2,1)} %collective-permute-done.23.refs_5_), channel_id=1, source_target_pairs={{0,16},{16,0},{1,17},{17,1},{2,18},{18,2},{3,19},{19,3},{4,20},{20... | collective-permute-start | bytes 1966088 | tf_op jit(solution)/shard_map/ppermute | solution.py:455
  125.6 24.5 %copy-start.6 = (bf16[64,5120]{1,0:T(8,128)(2,1)}, bf16[64,5120]{1,0:T(8,128)(2,1)S(1)}, u32[]{:S(2)}) copy-start(bf16[64,5120]{1,0:T(8,128)(2,1)S(1)} %collective-permute-done.11.refs_3_) | copy-start | bytes 1966084
  152.4 21.3 %all-to-all-start = ((bf16[16,16,768]{2,1,0:T(8,128)(2,1)}), bf16[16,16,768]{2,1,0:T(8,128)(2,1)}, u32[]{:S(2)}, u32[]{:S(2)}) async-start(bf16[16,16,768]{2,1,0:T(8,128)(2,1)} %bitcast.15), calls=%async_computation | async-start | bytes 786432 | tf_op jit(solution)/shard_map/all_to_all | solution.py:587
  159.4 20.7 %collective-permute-start.26 = (bf16[6,256,128]{2,1,0:T(8,128)(2,1)}, bf16[6,256,128]{2,1,0:T(8,128)(2,1)}, u32[]{:S(2)}, u32[]{:S(2)}) collective-permute-start(bf16[6,256,128]{2,1,0:T(8,128)(2,1)} %copy-done.33), channel_id=1, source_target_pairs={{0,1},{1,0},{2,3},{3,2},{4,5},{5,4},{6,7},{7,6},{8,9},{9,8},{10,11... | collective-permute-start | bytes 1179656 | tf_op jit(solution)/shard_map/ppermute | solution.py:455
  173.6 12.8 %all-to-all-start.1 = ((bf16[16,16,256]{2,1,0:T(8,128)(2,1)}), bf16[16,16,256]{2,1,0:T(8,128)(2,1)S(1)}, u32[]{:S(2)}, u32[]{:S(2)}) async-start(bf16[16,16,256]{2,1,0:T(8,128)(2,1)} %bitcast.16), calls=%async_computation.1 | async-start | bytes 262144 | tf_op jit(solution)/shard_map/all_to_all | solution.py:587
  178.5 1.7 collective-permute-start.27
  (25 other events, 52.5 us)
where the time goes:
time: 189 us; the launch traced here: 188 us
  waiting for transfers between devices  89 us (47%)
  Pallas kernels  39.2 us (21%)
  starting transfers between devices  33 us (17%)
  local copies, waits for them, and re-layouts  21.8 us (12%)
  other arithmetic  4.33 us (2%)
    ppermute x28, waiting for transfers between devices, send(): return lax.ppermute(value, axis, pairs)  86.9 us
    pallas_call x8, Pallas kernels, call_kernel(): pl.pallas_call(body, out_shape=outs, grid=(1,) if specs else (), in_specs...  39.2 us
    ppermute x28, starting transfers between devices, send(): return lax.ppermute(value, axis, pairs)  22.9 us
    unnamed x84, local copies, waits for them, and re-layouts  17.6 us
    all_to_all x2, starting transfers between devices, permuted(): lax.all_to_all(outgoing, 'tok', split_axis=0, concat_axis=0, tiled=True)  10.1 us
  transfers between devices with their start and end apart: 30, of which 11 were waited for; matrix products, arithmetic and copies ran while one was open for 5% of the time, Pallas kernels for 20%

commit v1 on v0

--- a/solution.py
+++ b/solution.py
@@ -311,36 +311,50 @@
     return total
 
 
-def project_body(*refs, sizes, first):
-    inputs = 4 + sum(sizes)
-    sources, (bias, cosine, sine, place) = refs[:inputs], refs[inputs : inputs + 4]
-    out_own, out_other, out_image = refs[inputs + 4 : inputs + 7]
-    rows, held, arrived = refs[inputs + 7], refs[inputs + 8 : -1], refs[-1]
-    targets, begin = [], 0
-    for source in sources[:4]:
-        targets.append(rows.at[begin : begin + source.shape[0]])
-        begin += source.shape[0]
-    copies = [
-        pltpu.make_async_copy(source, target, arrived.at[number])
-        for number, (source, target) in enumerate(zip(sources, targets + list(held)))
-    ]
-    for copy in copies:
-        copy.start()
+def project_body(*refs, levels, sizes, fresh, carried):
+    core, line, floor = places()
     side = lax.axis_index("groups")
-    core, line, floor = places()
     rings = lax.axis_size("tok") // 4
-    count = sources[0].shape[0]
-    for copy in copies[:4]:
-        copy.wait()
+    refs = list(refs)
+    sources = [refs.pop(0) for _ in range(4 if fresh else 1)]
+    pieces = [refs.pop(0) for _ in range(sum(sizes))]
+    earlier = refs.pop(0) if carried else None
+    bias, cosine, sine, place, out_own, out_other, out_image = [refs.pop(0) for _ in range(7)]
+    copies = []
+    if fresh:
+        rows, held, arrived = refs[0], refs[1:-1], refs[-1]
+        targets, begin = [], 0
+        for source in sources:
+            targets.append(rows.at[begin : begin + source.shape[0]])
+            begin += source.shape[0]
+        copies = [
+            pltpu.make_async_copy(source, target, arrived.at[number])
+            for number, (source, target) in enumerate(
+                zip(sources + pieces, targets + list(held))
+            )
+        ]
+        for copy in copies:
+            copy.start()
+        for copy in copies[:4]:
+            copy.wait()
+        pieces = held
+    else:
+        rows = sources[0]
+    shift = 0
+    if carried:
+        shift = earlier.shape[1]
+        out_image[:, :shift] = earlier[...]
+    count = out_own.shape[1]
     begin = 0
     for number, size in enumerate(sizes):
-        pieces = held[begin : begin + size]
-        for piece in range(begin, begin + size):
-            copies[4 + piece].wait()
+        mine = pieces[begin : begin + size]
+        if fresh:
+            for piece in range(begin, begin + size):
+                copies[4 + piece].wait()
         begin += size
-        values = pair_product(side, rows, pieces)
+        values = pair_product(side, rows, mine)
         for part in range(2):
-            block = lax.rem(floor - first - number + rings, rings) * 4
+            block = lax.rem(floor - levels[number] + rings, rings) * 4
             block = block + (line ^ part) * 2 + core
             key = block < KV_HEADS
             lanes = pl.ds(pl.multiple_of(block * LM_HEAD, LM_HEAD), LM_HEAD)
@@ -356,20 +370,20 @@
             values[2 * count :].astype(jnp.bfloat16),
             preferred_element_type=jnp.float32,
         )
-        out_image[:, number * 2 * LM_HEAD : (number + 1) * 2 * LM_HEAD] = placed.astype(
-            jnp.bfloat16
-        )
-
-
-def text_cache_body(*refs):
+        lanes = slice(shift + number * 2 * LM_HEAD, shift + (number + 1) * 2 * LM_HEAD)
+        out_image[:, lanes] = placed.astype(jnp.bfloat16)
+
+
+def text_cache_body(*refs, levels):
     pieces, out = refs[:-1], refs[-1]
     core, line, floor = places()
     rings = lax.axis_size("tok") // 4
-    for parity, stacks in ((core, pieces[: len(pieces) // 2]), (1 - core, pieces[len(pieces) // 2 :])):
+    half = len(pieces) // 2
+    for parity, stacks in ((core, pieces[:half]), (1 - core, pieces[half:])):
         number = 0
         for stack in stacks:
             for index in range(stack.shape[0]):
-                block = lax.rem(floor - number // 2 + rings, rings) * 4
+                block = lax.rem(floor - levels[number // 2] + rings, rings) * 4
                 block = block + (line ^ (number % 2)) * 2 + parity
                 begin = pl.multiple_of(block * LM_HEAD, LM_HEAD)
                 out[:, pl.ds(begin, LM_HEAD)] = stack[index]
@@ -554,49 +568,68 @@
     bias = lm_kv_bias[None, :]
 
     blocks_own, blocks_other, arrivals = [], [], []
-    for number, chosen in enumerate((groups[:-1], groups[-1:])):
-        blocks = 2 * len(chosen)
-        sources = [normed_own, normed_other, normed_image, image_other]
-        sources += [piece for group in chosen for piece in group]
+    calls = [list(range(1, rings - 1)), [0], [rings - 1]]
+    row_sources = [normed_own, normed_other, normed_image, image_other]
+    row_total = 2 * (text_count + units)
+    rows, outgoing = None, None
+    for number, levels in enumerate(calls):
+        blocks = 2 * len(levels)
+        fresh, carried = number == 0, number == 1
+        pieces = [piece for level in levels for piece in groups[level]]
+        width = blocks * LM_HEAD + (outgoing.shape[1] if carried else 0)
         whole = pl.BlockSpec(memory_space=pltpu.VMEM)
-        kept, given, outgoing = call_kernel(
+        outs = [jax.ShapeDtypeStruct((blocks, text_count, LM_HEAD), bf16)] * 2
+        outs += [jax.ShapeDtypeStruct((2 * slot_count, width), bf16)]
+        inputs = [rows] + pieces + ([outgoing] if carried else [])
+        specs, scratch = None, ()
+        if fresh:
+            outs += [jax.ShapeDtypeStruct((row_total, lm_width), bf16)]
+            inputs = row_sources + pieces
+            specs = [pl.BlockSpec(memory_space=pl.ANY)] * len(inputs) + [whole] * 4
+            scratch = [pltpu.VMEM(piece.shape, bf16) for piece in pieces]
+            scratch += [pltpu.SemaphoreType.DMA((len(inputs),))]
+        results = call_kernel(
             functools.partial(
                 project_body,
-                sizes=[len(group) for group in chosen],
-                first=0 if number == 0 else rings - 1,
+                levels=levels,
+                sizes=[len(groups[level]) for level in levels],
+                fresh=fresh,
+                carried=carried,
             ),
-            [jax.ShapeDtypeStruct((blocks, text_count, LM_HEAD), bf16)] * 2
-            + [jax.ShapeDtypeStruct((2 * slot_count, blocks * LM_HEAD), bf16)],
-            *sources,
+            outs,
+            *inputs,
             bias,
             cosine,
             sine,
             place,
-            specs=[pl.BlockSpec(memory_space=pl.ANY)] * len(sources) + [whole] * 4,
-            scratch=[pltpu.VMEM((2 * (text_count + units), lm_width), bf16)]
-            + [pltpu.VMEM(source.shape, bf16) for source in sources[4:]]
-            + [pltpu.SemaphoreType.DMA((len(sources),))],
-            limit=24,
+            specs=specs,
+            scratch=scratch,
+            limit=24 if fresh else 16,
             cost=(
-                4 * (text_count + units) * lm_width * LM_HEAD * blocks,
-                4 * text_count * lm_width + 2 * lm_width * LM_HEAD * blocks,
+                2 * row_total * lm_width * LM_HEAD * blocks,
+                2 * row_total * lm_width + 2 * lm_width * LM_HEAD * blocks,
             ),
         )
+        kept, given, outgoing = results[:3]
+        rows = results[3] if fresh else rows
         blocks_own.append(kept)
         blocks_other.append(send(given, sibling))
+        if number == 0:
+            continue
         arrived = lax.all_to_all(outgoing, "tok", split_axis=0, concat_axis=0, tiled=True)
         arrivals.append(arrived.reshape(count, 2 * capacity, -1))
 
+    levels = sum(calls, [])
     text_cache = call_kernel(
-        text_cache_body,
+        functools.partial(text_cache_body, levels=levels),
         jax.ShapeDtypeStruct((text_count, count * LM_HEAD), bf16),
         *blocks_own,
         *blocks_other,
     )
     orders = [
         [
-            (source // 4 - step) % rings * 4 + (source // 2 % 2 ^ part) * 2 + source % 2
-            for step in range(rings)
+            (source // 4 - level) % rings * 4 + (source // 2 % 2 ^ part) * 2 + source % 2
+            for level in levels
             for part in range(2)
         ]
         for source in range(count)

time: 189 us -> 183 us (0.968)
  the two profiles are of different devices: /device:TPU:0 before, /device:TPU:9 now
where the time goes in v1:
time: 183 us; the launch traced here: 179 us
  waiting for transfers between devices  64.6 us (35%)
  starting transfers between devices  56.5 us (31%)
  Pallas kernels  38.7 us (21%)
  local copies, waits for them, and re-layouts  16.5 us (9%)
  other arithmetic  1.89 us (1%)
    ppermute x29, waiting for transfers between devices, send(): return lax.ppermute(value, axis, pairs)  60.5 us
    ppermute x29, starting transfers between devices, send(): return lax.ppermute(value, axis, pairs)  43.5 us
    pallas_call x9, Pallas kernels, call_kernel(): pl.pallas_call(body, out_shape=outs, grid=(1,) if specs else (), in_specs...  38.7 us
    unnamed x66, local copies, waits for them, and re-layouts  14 us
    all_to_all x2, starting transfers between devices, permuted(): lax.all_to_all(outgoing, 'tok', split_axis=0, concat_axis=0, tiled=True)  13 us
    all_to_all x2, waiting for transfers between devices, permuted(): lax.all_to_all(outgoing, 'tok', split_axis=0, concat_axis=0, tiled=True)  4.1 us
  transfers between devices with their start and end apart: 31, of which 11 were waited for; matrix products, arithmetic and copies ran while one was open for 2% of the time, Pallas kernels for 21%

profile of v1, /device:TPU:9, one launch (start us, length us, event | category | flops | bytes accessed | tf_op | source)
XLA Modules:
  0.0 179.3 jit_solution(9507055593499076964)
XLA Ops:
  0.6 1.3 collective-permute-start.3
  1.9 2.4 %fusion.8 = (bf16[2,128,1280]{2,1,0:T(8,128)(2,1)}, bf16[2,128,1280]{2,1,0:T(8,128)(2,1)}) fusion(bf16[2,256,1280]{2,1,0:T(8,128)(2,1)} %own.3), kind=kLoop, calls=%fused_computation.34 | loop fusion | bytes 2621440 | tf_op jit(solution)/shard_map/slice | solution.py:491
  4.4 3.1 %collective-permute-start.1 = (bf16[2,128,1280]{2,1,0:T(8,128)(2,1)}, bf16[2,128,1280]{2,1,0:T(8,128)(2,1)}, u32[]{:S(2)}, u32[]{:S(2)}) collective-permute-start(bf16[2,128,1280]{2,1,0:T(8,128)(2,1)} %get-tuple-element.23), channel_id=1, source_target_pairs={{0,1},{1,2},{2,3},{3,4},{4,5},{5,6},{6,7},{7,8},{8,9},{9,10},{10,1... | collective-permute-start | bytes 1966088 | tf_op jit(solution)/shard_map/ppermute | solution.py:469
  7.5 1.9 %collective-permute-start.2 = (bf16[2,128,1280]{2,1,0:T(8,128)(2,1)}, bf16[2,128,1280]{2,1,0:T(8,128)(2,1)}, u32[]{:S(2)}, u32[]{:S(2)}) collective-permute-start(bf16[2,128,1280]{2,1,0:T(8,128)(2,1)} %get-tuple-element.22), channel_id=1, source_target_pairs={{1,0},{2,1},{3,2},{4,3},{5,4},{6,5},{7,6},{8,7},{9,8},{10,9},{11,1... | collective-permute-start | bytes 1966088 | tf_op jit(solution)/shard_map/ppermute | solution.py:469
  9.5 1.3 collective-permute-start.12
  10.9 1.3 collective-permute-start.4
  12.3 3.1 %collective-permute-start.20 = (s32[320]{0:T(512)S(1)}, s32[320]{0:T(512)S(1)}, u32[]{:S(2)}, u32[]{:S(2)}) collective-permute-start(s32[320]{0:T(512)S(1)} %pad_add_fusion), channel_id=1, source_target_pairs={{0,1},{1,0},{2,3},{3,2},{4,5},{5,4},{6,7},{7,6},{8,9},{9,8},{10,11... | collective-permute-start | bytes 3848 | tf_op jit(solution)/shard_map/ppermute | solution.py:469
  15.4 0.8 collective-permute-done.20
  16.6 15.5 %collective-permute-done.4.refs_1_ = bf16[2,80,1280]{2,1,0:T(8,128)(2,1)S(1)} collective-permute-done((bf16[2,80,1280]{2,1,0:T(8,128)(2,1)S(1)}, bf16[2,80,1280]{2,1,0:T(8,128)(2,1)S(1)}, u32[]{:S(2)}, u32[]{:S(2)}) %collective-permute-start.4) | collective-permute-done | bytes 409632 | tf_op jit(solution)/shard_map/ppermute | solution.py:469
  32.1 1.3 collective-permute-start.5
  33.4 1.7 copy-done.3
  35.2 2.9 %shard_map.140.refs_0_ = bf16[256,5120]{1,0:T(8,128)(2,1)} custom-call(bf16[256,5120]{1,0:T(8,128)(2,1)S(1)} %copy-done.3, f32[1,5120]{1,0:T(1,128)S(1)} %bitcast.17), custom_call_target="tpu_custom_call" | custom-call | flops 10485760 | bytes 5242880 | tf_op jit(solution)/shard_map/pallas_call | solution.py:182
  38.1 0.8 copy-done.6
  38.8 3.9 %collective-permute-start = (bf16[256,5120]{1,0:T(8,128)(2,1)}, bf16[256,5120]{1,0:T(8,128)(2,1)}, u32[]{:S(2)}, u32[]{:S(2)}) collective-permute-start(bf16[256,5120]{1,0:T(8,128)(2,1)} %shard_map.140.refs_0_), channel_id=1, source_target_pairs={{0,1},{1,0},{2,3},{3,2},{4,5},{5,4},{6,7},{7,6},{8,9},{9,8},{10,11... | collective-permute-start | bytes 7864328 | tf_op jit(solution)/shard_map/ppermute | solution.py:469
  42.8 10.5 %collective-permute-start.16 = (bf16[2560,128]{1,0:T(8,128)(2,1)}, bf16[2560,128]{1,0:T(8,128)(2,1)}, u32[]{:S(2)}, u32[]{:S(2)}) collective-permute-start(bf16[2560,128]{1,0:T(8,128)(2,1)} %collective-permute-done.12.refs_4_), channel_id=1, source_target_pairs={{0,4},{1,5},{2,6},{3,7},{4,8},{5,9},{6,10},{7,11},{8,12},{9,13},{1... | collective-permute-start | bytes 1966088 | tf_op jit(solution)/shard_map/ppermute | solution.py:469
  53.6 4.0 %collective-permute-start.6 = (bf16[2,80,1280]{2,1,0:T(8,128)(2,1)}, bf16[2,80,1280]{2,1,0:T(8,128)(2,1)}, u32[]{:S(2)}, u32[]{:S(2)}) collective-permute-start(bf16[2,80,1280]{2,1,0:T(8,128)(2,1)} %collective-permute-done.5.refs_2_), channel_id=1, source_target_pairs={{0,4},{1,5},{2,6},{3,7},{4,8},{5,9},{6,10},{7,11},{8,12},{9,13},{1... | collective-permute-start | bytes 1228808 | tf_op jit(solution)/shard_map/ppermute | solution.py:469
  57.6 0.8 copy-done.8
  58.4 1.2 collective-permute-start.14
  59.6 10.4 %collective-permute-done.16.refs_8_ = bf16[2560,128]{1,0:T(8,128)(2,1)} collective-permute-done((bf16[2560,128]{1,0:T(8,128)(2,1)}, bf16[2560,128]{1,0:T(8,128)(2,1)}, u32[]{:S(2)}, u32[]{:S(2)}) %collective-permute-start.16) | collective-permute-done | bytes 655392 | tf_op jit(solution)/shard_map/ppermute | solution.py:469
  70.0 0.8 collective-permute-start.9
  70.8 8.0 %collective-permute-done.6.refs_3_ = bf16[2,80,1280]{2,1,0:T(8,128)(2,1)} collective-permute-done((bf16[2,80,1280]{2,1,0:T(8,128)(2,1)}, bf16[2,80,1280]{2,1,0:T(8,128)(2,1)}, u32[]{:S(2)}, u32[]{:S(2)}) %collective-permute-start.6) | collective-permute-done | bytes 409632 | tf_op jit(solution)/shard_map/ppermute | solution.py:469
  79.6 1.3 collective-permute-start.18
  80.9 0.7 copy-done.10
  81.6 1.9 %collective-permute-start.22 = (bf16[2560,128]{1,0:T(8,128)(2,1)}, bf16[2560,128]{1,0:T(8,128)(2,1)}, u32[]{:S(2)}, u32[]{:S(2)}) collective-permute-start(bf16[2560,128]{1,0:T(8,128)(2,1)} %collective-permute-done.16.refs_8_), channel_id=1, source_target_pairs={{0,4},{1,5},{2,6},{3,7},{4,8},{5,9},{6,10},{7,11},{8,12},{9,13},{1... | collective-permute-start | bytes 1966088 | tf_op jit(solution)/shard_map/ppermute | solution.py:469
  83.5 0.7 copy-done.12
  84.7 2.7 %collective-permute-done.17.refs_9_ = bf16[2560,128]{1,0:T(8,128)(2,1)} collective-permute-done((bf16[2560,128]{1,0:T(8,128)(2,1)}, bf16[2560,128]{1,0:T(8,128)(2,1)}, u32[]{:S(2)}, u32[]{:S(2)}) %collective-permute-start.17) | collective-permute-done | bytes 655392 | tf_op jit(solution)/shard_map/ppermute | solution.py:469
  87.5 1.1 copy-done.22
  88.6 6.7 %shard_map.141.first = bf16[256,640]{1,0:T(8,128)(2,1)S(1)} custom-call(bf16[256,1280]{1,0:T(8,128)(2,1)S(1)} %copy-done.22, bf16[2,256,1280]{2,1,0:T(8,128)(2,1)S(1)} %copy-done.4, bf16[2,128,1280]{2,1,0:T(8,128)(2,1)} %collective-permute-done.1.low, bf16[2,128,1280]{2,1,0:T(8,128)(2,1)} %collective-permute-done.2.high, s32[1,48]{1,0:T(1,128)S(1)} %bitcast.23), custom_call_target="tpu_custom_call" | custom-call | flops 1006632960 | bytes 1310720 | tf_op jit(solution)/shard_map/pallas_call | solution.py:182
  95.3 6.8 %shard_map.142.second = bf16[256,640]{1,0:T(8,128)(2,1)S(1)} custom-call(bf16[256,1280]{1,0:T(8,128)(2,1)S(1)} %copy-done.23, bf16[2,256,1280]{2,1,0:T(8,128)(2,1)S(1)} %copy-done.4, bf16[2,128,1280]{2,1,0:T(8,128)(2,1)} %collective-permute-done.1.low, bf16[2,128,1280]{2,1,0:T(8,128)(2,1)} %collective-permute-done.2.high, s32[1,48]{1,0:T(1,128)S(1)} %bitcast.24), custom_call_target="tpu_custom_call" | custom-call | flops 1006632960 | bytes 1310720 | tf_op jit(solution)/shard_map/pallas_call | solution.py:182
  102.1 2.8 %shard_map.143.refs_2_ = bf16[64,5120]{1,0:T(8,128)(2,1)S(1)} custom-call(bf16[256,640]{1,0:T(8,128)(2,1)S(1)} %shard_map.141.first, bf16[256,640]{1,0:T(8,128)(2,1)S(1)} %shard_map.142.second, bf16[2,80,1280]{2,1,0:T(8,128)(2,1)S(1)} %pad_maximum_fusion.refs_0_, bf16[2,80,1280]{2,1,0:T(8,128)(2,1)S(1)} %collective-permute-done.4.refs_1_, ...), custom_call_target="tpu_custom_call" | custom-call | flops 838860800 | bytes 3276800 | tf_op jit(solution)/shard_map/pallas_call | solution.py:182
  104.9 1.2 collective-permute-start.11
  106.1 4.2 %collective-permute-done.15.refs_7_ = bf16[2560,128]{1,0:T(8,128)(2,1)} collective-permute-done((bf16[2560,128]{1,0:T(8,128)(2,1)}, bf16[2560,128]{1,0:T(8,128)(2,1)}, u32[]{:S(2)}, u32[]{:S(2)}) %collective-permute-start.15) | collective-permute-done | bytes 655392 | tf_op jit(solution)/shard_map/ppermute | solution.py:469
  110.3 1.2 collective-permute-start.19
  111.6 1.0 fusion.2
  113.0 17.9 %collective-permute-done.23.refs_2_ = bf16[2560,128]{1,0:T(8,128)(2,1)S(1)} collective-permute-done((bf16[2560,128]{1,0:T(8,128)(2,1)}, bf16[2560,128]{1,0:T(8,128)(2,1)S(1)}, u32[]{:S(2)}, u32[]{:S(2)}) %collective-permute-start.23) | collective-permute-done | bytes 655392 | tf_op jit(solution)/shard_map/ppermute | solution.py:469
  130.9 1.2 collective-permute-start.25
  132.1 10.9 %shard_map.144 = (bf16[4,256,128]{2,1,0:T(8,128)(2,1)S(1)}, bf16[4,256,128]{2,1,0:T(8,128)(2,1)S(1)}, bf16[256,512]{1,0:T(8,128)(2,1)S(1)}, bf16[640,5120]{1,0:T(8,128)(2,1)S(1)}) custom-call(bf16[256,5120]{1,0:T(8,128)(2,1)} %shard_map.140.refs_0_, bf16[256,5120]{1,0:T(8,128)(2,1)} %collective-permute-done.refs_1_, ...), custom_call_target="tpu_custom_call" | custom-call | flops 3355443200 | bytes 11796480 | tf_op jit(solution)/shard_map/pallas_call | solution.py:182
  143.0 2.1 %shard_map.145 = (bf16[2,256,128]{2,1,0:T(8,128)(2,1)S(1)}, bf16[2,256,128]{2,1,0:T(8,128)(2,1)S(1)}, bf16[256,768]{1,0:T(8,128)(2,1)S(1)}) custom-call(bf16[640,5120]{1,0:T(8,128)(2,1)S(1)} %get-tuple-element.13.refs_0_, bf16[5120,128]{1,0:T(8,128)(2,1)S(1)} %copy-done.2, bf16[5120,128]{1,0:T(8,128)(2,1)S(1)} %collective-permute-done.21.refs_2_, ...), custom_call_target="tpu_custom_call" | custom-call | flops 1677721600 | bytes 9175040 | tf_op jit(solution)/shard_map/pallas_call | solution.py:182
  145.9 0.7 copy-done.14
  147.9 8.8 %all-to-all-start = ((bf16[16,16,768]{2,1,0:T(8,128)(2,1)}), bf16[16,16,768]{2,1,0:T(8,128)(2,1)S(1)}, u32[]{:S(2)}, u32[]{:S(2)}) async-start(bf16[16,16,768]{2,1,0:T(8,128)(2,1)} %bitcast.15), calls=%async_computation | async-start | bytes 786432 | tf_op jit(solution)/shard_map/all_to_all | solution.py:619
  157.2 2.9 %copy-done.1 = bf16[640,5120]{1,0:T(8,128)(2,1)S(1)} copy-done((bf16[640,5120]{1,0:T(8,128)(2,1)S(1)}, bf16[640,5120]{1,0:T(8,128)(2,1)}, u32[]{:S(2)}) %copy-start.1) | copy-done | bytes 6553624
  160.0 3.4 %shard_map.146 = (bf16[2,256,128]{2,1,0:T(8,128)(2,1)S(1)}, bf16[2,256,128]{2,1,0:T(8,128)(2,1)S(1)}, bf16[256,256]{1,0:T(8,128)(2,1)S(1)}) custom-call(bf16[640,5120]{1,0:T(8,128)(2,1)S(1)} %copy-done.1, bf16[2560,128]{1,0:T(8,128)(2,1)} %collective-permute-done.22.refs_1_, bf16[2560,128]{1,0:T(8,128)(2,1)S(1)} %collective-permute-done.23.refs_2_, ...), custom_call_target="tpu_custom_call" | custom-call | flops 1677721600 | bytes 9175040 | tf_op jit(solution)/shard_map/pallas_call | solution.py:182
  164.1 4.0 %all-to-all-done.refs_0_ = bf16[16,16,768]{2,1,0:T(8,128)(2,1)S(1)} async-done(((bf16[16,16,768]{2,1,0:T(8,128)(2,1)}), bf16[16,16,768]{2,1,0:T(8,128)(2,1)S(1)}, u32[]{:S(2)}, u32[]{:S(2)}) %all-to-all-start) | async-done | bytes 393248 | tf_op jit(solution)/shard_map/all_to_all | solution.py:619
  168.1 4.2 %all-to-all-start.1 = ((bf16[16,16,256]{2,1,0:T(8,128)(2,1)}), bf16[16,16,256]{2,1,0:T(8,128)(2,1)S(1)}, u32[]{:S(2)}, u32[]{:S(2)}) async-start(bf16[16,16,256]{2,1,0:T(8,128)(2,1)} %bitcast.16), calls=%async_computation.1 | async-start | bytes 262144 | tf_op jit(solution)/shard_map/all_to_all | solution.py:619
  174.2 0.9 copy-done.16
  175.1 0.9 copy-done.18
  176.0 2.2 %shard_map.147 = bf16[256,2048]{1,0:T(8,128)(2,1)} custom-call(bf16[4,256,128]{2,1,0:T(8,128)(2,1)S(1)} %get-tuple-element.12.refs_0_, bf16[2,256,128]{2,1,0:T(8,128)(2,1)S(1)} %copy-done.16, bf16[2,256,128]{2,1,0:T(8,128)(2,1)S(1)} %copy-done.18, bf16[4,256,128]{2,1,0:T(8,128)(2,1)} %collective-permute-done.26.refs_3_, ...), custom_call_target="tpu_custom_call" | custom-call | tf_op jit(solution)/shard_map/pallas_call | solution.py:182
  178.3 1.0 shard_map.148
  (112 shorter events, 7.7 us)
Async XLA Ops:
  0.6 8.8 %copy-start.2 = (bf16[5120,128]{1,0:T(8,128)(2,1)S(1)}, bf16[5120,128]{1,0:T(8,128)(2,1)}, u32[]{:S(2)}) copy-start(bf16[5120,128]{1,0:T(8,128)(2,1)} %refs_1_.1) | copy-start | bytes 3932164
  0.6 10.2 %collective-permute-start.3 = (bf16[80,1280]{1,0:T(8,128)(2,1)}, bf16[80,1280]{1,0:T(8,128)(2,1)S(1)}, u32[]{:S(2)}, u32[]{:S(2)}) collective-permute-start(bf16[80,1280]{1,0:T(8,128)(2,1)} %param.16), channel_id=1, source_target_pairs={{0,2},{1,3},{2,0},{3,1},{4,6},{5,7},{6,4},{7,5},{8,10},{9,11},{10,... | collective-permute-start | bytes 614408 | tf_op jit(solution)/shard_map/ppermute | solution.py:469
  4.4 7.9 %copy-start.29 = (s32[256]{0:T(256)S(1)}, s32[256]{0:T(256)}, u32[]{:S(2)}) copy-start(s32[256]{0:T(256)} %param.23) | copy-start | bytes 3076
  4.4 7.9 %copy-start.32 = (s32[64,1]{0,1:T(1,128)S(1)}, s32[64,1]{0,1:T(1,128)}, u32[]{:S(2)}) copy-start(s32[64,1]{0,1:T(1,128)} %param.24) | copy-start | bytes 772
  4.4 29.0 %copy-start.20 = (f32[5120]{0:T(1024)S(1)}, f32[5120]{0:T(1024)}, u32[]{:S(2)}) copy-start(f32[5120]{0:T(1024)} %param.20) | copy-start | bytes 61444
  4.4 48.8 %collective-permute-start.1 = (bf16[2,128,1280]{2,1,0:T(8,128)(2,1)}, bf16[2,128,1280]{2,1,0:T(8,128)(2,1)}, u32[]{:S(2)}, u32[]{:S(2)}) collective-permute-start(bf16[2,128,1280]{2,1,0:T(8,128)(2,1)} %get-tuple-element.23), channel_id=1, source_target_pairs={{0,1},{1,2},{2,3},{3,4},{4,5},{5,6},{6,7},{7,8},{8,9},{9,10},{10,1... | collective-permute-start | bytes 1966088 | tf_op jit(solution)/shard_map/ppermute | solution.py:469
  7.5 45.7 %collective-permute-start.2 = (bf16[2,128,1280]{2,1,0:T(8,128)(2,1)}, bf16[2,128,1280]{2,1,0:T(8,128)(2,1)}, u32[]{:S(2)}, u32[]{:S(2)}) collective-permute-start(bf16[2,128,1280]{2,1,0:T(8,128)(2,1)} %get-tuple-element.22), channel_id=1, source_target_pairs={{1,0},{2,1},{3,2},{4,3},{5,4},{6,5},{7,6},{8,7},{9,8},{10,9},{11,1... | collective-permute-start | bytes 1966088 | tf_op jit(solution)/shard_map/ppermute | solution.py:469
  9.5 33.3 %collective-permute-start.12 = (bf16[2560,128]{1,0:T(8,128)(2,1)S(1)}, bf16[2560,128]{1,0:T(8,128)(2,1)}, u32[]{:S(2)}, u32[]{:S(2)}) collective-permute-start(bf16[2560,128]{1,0:T(8,128)(2,1)S(1)} %constant_dynamic-slice_fusion), channel_id=1, source_target_pairs={{0,4},{1,5},{2,6},{3,7},{4,8},{5,9},{6,10},{7,11},{8,12},{9,13},{1... | collective-permute-start | bytes 1966088 | tf_op jit(solution)/shard_map/ppermute | solution.py:469
  10.9 21.2 %collective-permute-start.4 = (bf16[2,80,1280]{2,1,0:T(8,128)(2,1)S(1)}, bf16[2,80,1280]{2,1,0:T(8,128)(2,1)S(1)}, u32[]{:S(2)}, u32[]{:S(2)}) collective-permute-start(bf16[2,80,1280]{2,1,0:T(8,128)(2,1)S(1)} %pad_maximum_fusion.refs_0_), channel_id=1, source_target_pairs={{0,4},{1,5},{2,6},{3,7},{4,8},{5,9},{6,10},{7,11},{8,12},{9,13},{1... | collective-permute-start | bytes 1228808 | tf_op jit(solution)/shard_map/ppermute | solution.py:469
  12.3 4.0 %collective-permute-start.20 = (s32[320]{0:T(512)S(1)}, s32[320]{0:T(512)S(1)}, u32[]{:S(2)}, u32[]{:S(2)}) collective-permute-start(s32[320]{0:T(512)S(1)} %pad_add_fusion), channel_id=1, source_target_pairs={{0,1},{1,0},{2,3},{3,2},{4,5},{5,4},{6,7},{7,6},{8,9},{9,8},{10,11... | collective-permute-start | bytes 3848 | tf_op jit(solution)/shard_map/ppermute | solution.py:469
  16.2 71.2 %copy-start.30 = (s32[320]{0:T(512)}, s32[320]{0:T(512)S(1)}, u32[]{:S(2)}) copy-start(s32[320]{0:T(512)S(1)} %collective-permute-done.20) | copy-start | bytes 3844
  16.2 21.8 %collective-permute-start.7 = (bf16[2,80,1280]{2,1,0:T(8,128)(2,1)S(1)}, bf16[2,80,1280]{2,1,0:T(8,128)(2,1)S(1)}, u32[]{:S(2)}, u32[]{:S(2)}) collective-permute-start(bf16[2,80,1280]{2,1,0:T(8,128)(2,1)S(1)} %pad_maximum_fusion.refs_0_), channel_id=1, source_target_pairs={{0,1},{1,0},{2,3},{3,2},{4,5},{5,4},{6,7},{7,6},{8,9},{9,8},{10,11... | collective-permute-start | bytes 1228808 | tf_op jit(solution)/shard_map/ppermute | solution.py:469
  32.1 21.5 %collective-permute-start.5 = (bf16[2,80,1280]{2,1,0:T(8,128)(2,1)S(1)}, bf16[2,80,1280]{2,1,0:T(8,128)(2,1)}, u32[]{:S(2)}, u32[]{:S(2)}) collective-permute-start(bf16[2,80,1280]{2,1,0:T(8,128)(2,1)S(1)} %collective-permute-done.4.refs_1_), channel_id=1, source_target_pairs={{0,4},{1,5},{2,6},{3,7},{4,8},{5,9},{6,10},{7,11},{8,12},{9,13},{1... | collective-permute-start | bytes 1228808 | tf_op jit(solution)/shard_map/ppermute | solution.py:469
  35.2 49.4 %copy-start.28 = (f32[1280]{0:T(1024)S(1)}, f32[1280]{0:T(1024)}, u32[]{:S(2)}) copy-start(f32[1280]{0:T(1024)} %param.17) | copy-start | bytes 15364
  35.2 52.3 %copy-start.4 = (bf16[2,256,1280]{2,1,0:T(8,128)(2,1)S(1)}, bf16[2,256,1280]{2,1,0:T(8,128)(2,1)}, u32[]{:S(2)}) copy-start(bf16[2,256,1280]{2,1,0:T(8,128)(2,1)} %own.3) | copy-start | bytes 3932164
  35.2 52.3 %copy-start.26 = (s32[48]{0:T(128)S(1)}, s32[48]{0:T(128)}, u32[]{:S(2)}) copy-start(s32[48]{0:T(128)} %param.18) | copy-start | bytes 580
  38.8 93.3 %collective-permute-start = (bf16[256,5120]{1,0:T(8,128)(2,1)}, bf16[256,5120]{1,0:T(8,128)(2,1)}, u32[]{:S(2)}, u32[]{:S(2)}) collective-permute-start(bf16[256,5120]{1,0:T(8,128)(2,1)} %shard_map.140.refs_0_), channel_id=1, source_target_pairs={{0,1},{1,0},{2,3},{3,2},{4,5},{5,4},{6,7},{7,6},{8,9},{9,8},{10,11... | collective-permute-start | bytes 7864328 | tf_op jit(solution)/shard_map/ppermute | solution.py:469
  42.8 27.2 %collective-permute-start.16 = (bf16[2560,128]{1,0:T(8,128)(2,1)}, bf16[2560,128]{1,0:T(8,128)(2,1)}, u32[]{:S(2)}, u32[]{:S(2)}) collective-permute-start(bf16[2560,128]{1,0:T(8,128)(2,1)} %collective-permute-done.12.refs_4_), channel_id=1, source_target_pairs={{0,4},{1,5},{2,6},{3,7},{4,8},{5,9},{6,10},{7,11},{8,12},{9,13},{1... | collective-permute-start | bytes 1966088 | tf_op jit(solution)/shard_map/ppermute | solution.py:469
  53.2 17.5 %collective-permute-start.13 = (bf16[2560,128]{1,0:T(8,128)(2,1)}, bf16[2560,128]{1,0:T(8,128)(2,1)}, u32[]{:S(2)}, u32[]{:S(2)}) collective-permute-start(bf16[2560,128]{1,0:T(8,128)(2,1)} %collective-permute-done.12.refs_4_), channel_id=1, source_target_pairs={{0,2},{1,3},{2,0},{3,1},{4,6},{5,7},{6,4},{7,5},{8,10},{9,11},{10,... | collective-permute-start | bytes 1966088 | tf_op jit(solution)/shard_map/ppermute | solution.py:469
  53.2 4.4 %collective-permute-start.8 = (bf16[2,80,1280]{2,1,0:T(8,128)(2,1)S(1)}, bf16[2,80,1280]{2,1,0:T(8,128)(2,1)S(1)}, u32[]{:S(2)}, u32[]{:S(2)}) collective-permute-start(bf16[2,80,1280]{2,1,0:T(8,128)(2,1)S(1)} %collective-permute-done.4.refs_1_), channel_id=1, source_target_pairs={{0,1},{1,0},{2,3},{3,2},{4,5},{5,4},{6,7},{7,6},{8,9},{9,8},{10,11... | collective-permute-start | bytes 1228808 | tf_op jit(solution)/shard_map/ppermute | solution.py:469
  53.6 25.2 %collective-permute-start.6 = (bf16[2,80,1280]{2,1,0:T(8,128)(2,1)}, bf16[2,80,1280]{2,1,0:T(8,128)(2,1)}, u32[]{:S(2)}, u32[]{:S(2)}) collective-permute-start(bf16[2,80,1280]{2,1,0:T(8,128)(2,1)} %collective-permute-done.5.refs_2_), channel_id=1, source_target_pairs={{0,4},{1,5},{2,6},{3,7},{4,8},{5,9},{6,10},{7,11},{8,12},{9,13},{1... | collective-permute-start | bytes 1228808 | tf_op jit(solution)/shard_map/ppermute | solution.py:469
  58.4 21.2 %collective-permute-start.14 = (bf16[2560,128]{1,0:T(8,128)(2,1)}, bf16[2560,128]{1,0:T(8,128)(2,1)}, u32[]{:S(2)}, u32[]{:S(2)}) collective-permute-start(bf16[2560,128]{1,0:T(8,128)(2,1)} %collective-permute-done.12.refs_4_), channel_id=1, source_target_pairs={{0,16},{16,0},{1,17},{17,1},{2,18},{18,2},{3,19},{19,3},{4,20},{20... | collective-permute-start | bytes 1966088 | tf_op jit(solution)/shard_map/ppermute | solution.py:469
  70.0 10.8 %collective-permute-start.9 = (bf16[2,80,1280]{2,1,0:T(8,128)(2,1)}, bf16[2,80,1280]{2,1,0:T(8,128)(2,1)S(1)}, u32[]{:S(2)}, u32[]{:S(2)}) collective-permute-start(bf16[2,80,1280]{2,1,0:T(8,128)(2,1)} %collective-permute-done.5.refs_2_), channel_id=1, source_target_pairs={{0,1},{1,0},{2,3},{3,2},{4,5},{5,4},{6,7},{7,6},{8,9},{9,8},{10,11... | collective-permute-start | bytes 1228808 | tf_op jit(solution)/shard_map/ppermute | solution.py:469
  70.8 16.6 %collective-permute-start.17 = (bf16[2560,128]{1,0:T(8,128)(2,1)}, bf16[2560,128]{1,0:T(8,128)(2,1)}, u32[]{:S(2)}, u32[]{:S(2)}) collective-permute-start(bf16[2560,128]{1,0:T(8,128)(2,1)} %collective-permute-done.16.refs_8_), channel_id=1, source_target_pairs={{0,2},{1,3},{2,0},{3,1},{4,6},{5,7},{6,4},{7,5},{8,10},{9,11},{10,... | collective-permute-start | bytes 1966088 | tf_op jit(solution)/shard_map/ppermute | solution.py:469
  78.8 4.7 %collective-permute-start.10 = (bf16[2,80,1280]{2,1,0:T(8,128)(2,1)}, bf16[2,80,1280]{2,1,0:T(8,128)(2,1)S(1)}, u32[]{:S(2)}, u32[]{:S(2)}) collective-permute-start(bf16[2,80,1280]{2,1,0:T(8,128)(2,1)} %collective-permute-done.6.refs_3_), channel_id=1, source_target_pairs={{0,1},{1,0},{2,3},{3,2},{4,5},{5,4},{6,7},{7,6},{8,9},{9,8},{10,11... | collective-permute-start | bytes 1228808 | tf_op jit(solution)/shard_map/ppermute | solution.py:469
  79.6 25.4 %collective-permute-start.18 = (bf16[2560,128]{1,0:T(8,128)(2,1)}, bf16[2560,128]{1,0:T(8,128)(2,1)}, u32[]{:S(2)}, u32[]{:S(2)}) collective-permute-start(bf16[2560,128]{1,0:T(8,128)(2,1)} %collective-permute-done.16.refs_8_), channel_id=1, source_target_pairs={{0,16},{16,0},{1,17},{17,1},{2,18},{18,2},{3,19},{19,3},{4,20},{20... | collective-permute-start | bytes 1966088 | tf_op jit(solution)/shard_map/ppermute | solution.py:469
  81.6 29.9 %collective-permute-start.22 = (bf16[2560,128]{1,0:T(8,128)(2,1)}, bf16[2560,128]{1,0:T(8,128)(2,1)}, u32[]{:S(2)}, u32[]{:S(2)}) collective-permute-start(bf16[2560,128]{1,0:T(8,128)(2,1)} %collective-permute-done.16.refs_8_), channel_id=1, source_target_pairs={{0,4},{1,5},{2,6},{3,7},{4,8},{5,9},{6,10},{7,11},{8,12},{9,13},{1... | collective-permute-start | bytes 1966088 | tf_op jit(solution)/shard_map/ppermute | solution.py:469
  84.3 26.0 %collective-permute-start.15 = (bf16[2560,128]{1,0:T(8,128)(2,1)}, bf16[2560,128]{1,0:T(8,128)(2,1)}, u32[]{:S(2)}, u32[]{:S(2)}) collective-permute-start(bf16[2560,128]{1,0:T(8,128)(2,1)} %collective-permute-done.13.refs_5_), channel_id=1, source_target_pairs={{0,16},{16,0},{1,17},{17,1},{2,18},{18,2},{3,19},{19,3},{4,20},{20... | collective-permute-start | bytes 1966088 | tf_op jit(solution)/shard_map/ppermute | solution.py:469
  87.4 55.6 %collective-permute-start.21 = (bf16[5120,128]{1,0:T(8,128)(2,1)S(1)}, bf16[5120,128]{1,0:T(8,128)(2,1)S(1)}, u32[]{:S(2)}, u32[]{:S(2)}) collective-permute-start(bf16[5120,128]{1,0:T(8,128)(2,1)S(1)} %copy-done.2), channel_id=1, source_target_pairs={{0,2},{1,3},{2,0},{3,1},{4,6},{5,7},{6,4},{7,5},{8,10},{9,11},{10,... | collective-permute-start | bytes 3932168 | tf_op jit(solution)/shard_map/ppermute | solution.py:469
  95.2 6.8 %copy-start.5 = (bf16[256,1280]{1,0:T(8,128)(2,1)S(1)}, bf16[256,1280]{1,0:T(8,128)(2,1)}, u32[]{:S(2)}) copy-start(bf16[256,1280]{1,0:T(8,128)(2,1)} %refs_9_.1) | copy-start | bytes 1966084
  95.2 6.8 %copy-start.7 = (bf16[2,80,1280]{2,1,0:T(8,128)(2,1)S(1)}, bf16[2,80,1280]{2,1,0:T(8,128)(2,1)}, u32[]{:S(2)}) copy-start(bf16[2,80,1280]{2,1,0:T(8,128)(2,1)} %copy-done.6) | copy-start | bytes 1228804
  95.3 6.8 %copy-start.9 = (bf16[2,80,1280]{2,1,0:T(8,128)(2,1)S(1)}, bf16[2,80,1280]{2,1,0:T(8,128)(2,1)}, u32[]{:S(2)}) copy-start(bf16[2,80,1280]{2,1,0:T(8,128)(2,1)} %copy-done.8) | copy-start | bytes 1228804
  95.3 6.8 %copy-start.11 = (bf16[2,80,1280]{2,1,0:T(8,128)(2,1)S(1)}, bf16[2,80,1280]{2,1,0:T(8,128)(2,1)}, u32[]{:S(2)}) copy-start(bf16[2,80,1280]{2,1,0:T(8,128)(2,1)} %copy-done.10) | copy-start | bytes 1228804
  95.3 6.8 %copy-start.13 = (bf16[2,80,1280]{2,1,0:T(8,128)(2,1)S(1)}, bf16[2,80,1280]{2,1,0:T(8,128)(2,1)}, u32[]{:S(2)}) copy-start(bf16[2,80,1280]{2,1,0:T(8,128)(2,1)} %copy-done.12) | copy-start | bytes 1228804
  102.1 9.5 %slice-start = ((s32[320]{0:T(512)}), s32[256]{0:T(256)S(1)}, s32[]{:S(2)}) async-start(s32[320]{0:T(512)} %copy-done.30), calls=%async_computation.2 | async-start | bytes 2048 | tf_op jit(solution)/shard_map/slice | solution.py:566
  102.1 30.0 %copy-start.21 = (f32[2048]{0:T(1024)S(1)}, f32[2048]{0:T(1024)}, u32[]{:S(2)}) copy-start(f32[2048]{0:T(1024)} %param.22) | copy-start | bytes 24580
  104.9 7.7 %collective-permute-start.11 = (bf16[64,5120]{1,0:T(8,128)(2,1)S(1)}, bf16[64,5120]{1,0:T(8,128)(2,1)S(1)}, u32[]{:S(2)}, u32[]{:S(2)}) collective-permute-start(bf16[64,5120]{1,0:T(8,128)(2,1)S(1)} %shard_map.143.refs_2_), channel_id=1, source_target_pairs={{0,1},{1,0},{2,3},{3,2},{4,5},{5,4},{6,7},{7,6},{8,9},{9,8},{10,11... | collective-permute-start | bytes 1966088 | tf_op jit(solution)/shard_map/ppermute | solution.py:469
  110.3 21.8 %collective-permute-start.19 = (bf16[2560,128]{1,0:T(8,128)(2,1)}, bf16[2560,128]{1,0:T(8,128)(2,1)S(1)}, u32[]{:S(2)}, u32[]{:S(2)}) collective-permute-start(bf16[2560,128]{1,0:T(8,128)(2,1)} %collective-permute-done.17.refs_9_), channel_id=1, source_target_pairs={{0,16},{16,0},{1,17},{17,1},{2,18},{18,2},{3,19},{19,3},{4,20},{20... | collective-permute-start | bytes 1966088 | tf_op jit(solution)/shard_map/ppermute | solution.py:469
  111.5 19.4 %collective-permute-start.23 = (bf16[2560,128]{1,0:T(8,128)(2,1)}, bf16[2560,128]{1,0:T(8,128)(2,1)S(1)}, u32[]{:S(2)}, u32[]{:S(2)}) collective-permute-start(bf16[2560,128]{1,0:T(8,128)(2,1)} %collective-permute-done.22.refs_1_), channel_id=1, source_target_pairs={{0,2},{1,3},{2,0},{3,1},{4,6},{5,7},{6,4},{7,5},{8,10},{9,11},{10,... | collective-permute-start | bytes 1966088 | tf_op jit(solution)/shard_map/ppermute | solution.py:469
  112.6 44.5 %collective-permute-start.24 = (bf16[2560,128]{1,0:T(8,128)(2,1)}, bf16[2560,128]{1,0:T(8,128)(2,1)S(1)}, u32[]{:S(2)}, u32[]{:S(2)}) collective-permute-start(bf16[2560,128]{1,0:T(8,128)(2,1)} %collective-permute-done.22.refs_1_), channel_id=1, source_target_pairs={{0,16},{16,0},{1,17},{17,1},{2,18},{18,2},{3,19},{19,3},{4,20},{20... | collective-permute-start | bytes 1966088 | tf_op jit(solution)/shard_map/ppermute | solution.py:469
  130.9 26.3 %collective-permute-start.25 = (bf16[2560,128]{1,0:T(8,128)(2,1)S(1)}, bf16[2560,128]{1,0:T(8,128)(2,1)}, u32[]{:S(2)}, u32[]{:S(2)}) collective-permute-start(bf16[2560,128]{1,0:T(8,128)(2,1)S(1)} %collective-permute-done.23.refs_2_), channel_id=1, source_target_pairs={{0,16},{16,0},{1,17},{17,1},{2,18},{18,2},{3,19},{19,3},{4,20},{20... | collective-permute-start | bytes 1966088 | tf_op jit(solution)/shard_map/ppermute | solution.py:469
  143.0 13.7 %copy-start.31 = (s32[3,128]{1,0:T(4,128)S(1)}, s32[3,128]{1,0:T(4,128)}, u32[]{:S(2)}) copy-start(s32[3,128]{1,0:T(4,128)} %param.25) | copy-start | bytes 4612
  147.9 20.2 %all-to-all-start = ((bf16[16,16,768]{2,1,0:T(8,128)(2,1)}), bf16[16,16,768]{2,1,0:T(8,128)(2,1)S(1)}, u32[]{:S(2)}, u32[]{:S(2)}) async-start(bf16[16,16,768]{2,1,0:T(8,128)(2,1)} %bitcast.15), calls=%async_computation | async-start | bytes 786432 | tf_op jit(solution)/shard_map/all_to_all | solution.py:619
  156.7 17.3 %collective-permute-start.26 = (bf16[4,256,128]{2,1,0:T(8,128)(2,1)}, bf16[4,256,128]{2,1,0:T(8,128)(2,1)}, u32[]{:S(2)}, u32[]{:S(2)}) collective-permute-start(bf16[4,256,128]{2,1,0:T(8,128)(2,1)} %copy-done.24), channel_id=1, source_target_pairs={{0,1},{1,0},{2,3},{3,2},{4,5},{5,4},{6,7},{7,6},{8,9},{9,8},{10,11... | collective-permute-start | bytes 786440 | tf_op jit(solution)/shard_map/ppermute | solution.py:469
  164.1 10.1 %copy-start.17 = (bf16[2,256,128]{2,1,0:T(8,128)(2,1)}, bf16[2,256,128]{2,1,0:T(8,128)(2,1)S(1)}, u32[]{:S(2)}) copy-start(bf16[2,256,128]{2,1,0:T(8,128)(2,1)S(1)} %get-tuple-element.16.refs_2_) | copy-start | bytes 393220
  168.1 10.2 %all-to-all-start.1 = ((bf16[16,16,256]{2,1,0:T(8,128)(2,1)}), bf16[16,16,256]{2,1,0:T(8,128)(2,1)S(1)}, u32[]{:S(2)}, u32[]{:S(2)}) async-start(bf16[16,16,256]{2,1,0:T(8,128)(2,1)} %bitcast.16), calls=%async_computation.1 | async-start | bytes 262144 | tf_op jit(solution)/shard_map/all_to_all | solution.py:619
  172.3 1.7 collective-permute-start.27
  172.8 1.4 collective-permute-start.28
  (17 other events, 31.9 us)
